TPU v7x, 512 devices: a whole 4x4x16 slice. The times are simulated.
512 devices in a mesh: group: 16 (over x, z_hi), shard: 32 (over z_lo, y, core).
Axes of the slice: x: 4, y: 4, z: 16 (z_hi: 4, z_lo: 4; z = z_hi * 4 + z_lo), core: 2. Of those that a mesh axis runs over, the one named last changes fastest.
Arguments:
- step_count: int32 [1], replicated, may hold values from 2 to 8
- block_order: int32 [224], replicated, may hold values from 0 to 223, as said below
- saved_tiles: bfloat16 [512, 4, 18, 18, 256], P(('group', 'shard')), may hold values from -6 to 6
- pre_act: bfloat16 [262144, 256], P(('group', 'shard')), may hold values from -6 to 6
- grad_output: bfloat16 [262144, 256], P(('group', 'shard')), may hold values from -0.0234375 to 0.0234375
- pointwise_live: bfloat16 [256, 256], replicated, may hold values from -0.375 to 0.375
- master_rows: float32 [7168, 256], P('shard'), may hold values from -0.25 to 0.25, as said below
- row_moment: float32 [7168], P('shard'), may hold values from 0.5 to 30, as said below
- col_moment: float32 [2, 256], replicated, may hold values from 0.03 to 0.3
- next_tiles: bfloat16 [512, 4, 18, 18, 256], P(('group', 'shard')), may hold values from -6 to 6
Outputs:
- update_rows: float32 [7168, 256], P('shard')
- new_master: float32 [7168, 256], P('shard')
- new_row_moment: float32 [7168], P('shard')
- new_col_moment: float32 [2, 256], replicated
- next_output: bfloat16 [262144, 256], P(('group', 'shard'))
Inputs may be any that keep to these rules, and one draw needn't show every extreme that they name: `block_order`: a permutation of 0 to 223. `master_rows`: rows of the 3x3x3 kernel are of order (6912) ** -0.5 and rows of the 1x1x1 kernel of order 256 ** -0.5. `row_moment`: positive row factors.
All inputs are finite; a program needn't handle non-finite values.
Results may differ from a plain program's by a relative error of at most 0.023.
Values may be sent and summed in bfloat16 or wider, within the bound.
A program may use at most 64 MiB of HBM per device.

v0:
```python
import jax
import jax.numpy as jnp
from jax import lax
from jax.sharding import PartitionSpec as P

CI = 256
CO = 256
BLK = 32
FR = 2
HW = 16
NB3 = 216
NB = 224


learn_rate = 0.002
decay_power = 0.8


def silu_slope(values):
    sigma = jax.nn.sigmoid(values)
    return sigma * (1.0 + values * (1.0 - sigma))


def tap_views(frames):
    views = []
    for frame_off in range(3):
        for row_off in range(3):
            for col_off in range(3):
                window = frames[
                    frame_off : frame_off + FR, row_off : row_off + HW, col_off : col_off + HW, :
                ]
                views.append(window.reshape(FR * HW * HW, CI))
    return views


def contract_rows(left, right):
    return lax.dot_general(
        left, right, (((0,), (0,)), ((), ())), preferred_element_type=jnp.float32
    )


def kernel_sums(values, is_small):
    large_part = jnp.sum(jnp.where(is_small[:, None], 0.0, values), axis=0)
    small_part = jnp.sum(jnp.where(is_small[:, None], values, 0.0), axis=0)
    return jnp.stack([large_part, small_part])


def shards(
    step_count,
    block_order,
    saved_tiles,
    pre_act,
    grad_output,
    pointwise_live,
    master_rows,
    row_moment,
    col_moment,
    next_tiles,
):
    pre_float = pre_act.astype(jnp.float32)
    activation = jax.nn.silu(pre_float).astype(jnp.bfloat16)
    grad_act = lax.dot_general(
        grad_output, pointwise_live, (((1,), (1,)), ((), ())), preferred_element_type=jnp.float32
    )
    grad_pre = (grad_act * silu_slope(pre_float)).astype(jnp.bfloat16)
    pieces = [contract_rows(view, grad_pre) for view in tap_views(saved_tiles[0])]
    pieces.append(contract_rows(activation, grad_output))
    own_term = jnp.concatenate(pieces, axis=0).astype(jnp.bfloat16)
    total_rows = NB * BLK
    stored = jnp.take(own_term.reshape(NB, BLK, CO), block_order, axis=0).reshape(total_rows, CO)
    own_rows = master_rows.shape[0]
    partial_value = lax.psum_scatter(stored, "shard", scatter_dimension=0, tiled=True).astype(
        jnp.float32
    )
    gradient = lax.psum(partial_value, "group")
    owner = lax.axis_index("shard")
    own_count = own_rows // BLK
    own_blocks = lax.dynamic_slice_in_dim(block_order, owner * own_count, own_count)
    is_small = jnp.repeat(own_blocks >= NB3, BLK, total_repeat_length=own_rows)
    decay_rate = 1.0 - step_count.astype(jnp.float32)[0] ** (-decay_power)
    counts = jnp.array([27 * CI, CO], jnp.float32)
    squares = gradient * gradient
    new_row = decay_rate * row_moment + (1.0 - decay_rate) * jnp.mean(squares, axis=1)
    col_part = kernel_sums(squares, is_small)
    row_part = kernel_sums(new_row[:, None], is_small)[:, 0]
    col_total, row_total = lax.psum((col_part, row_part), "shard")
    new_col = decay_rate * col_moment + (1.0 - decay_rate) * col_total / counts[:, None]
    row_mean = row_total / counts
    col_rows = jnp.where(is_small[:, None], new_col[1], new_col[0])
    mean_rows = jnp.where(is_small, row_mean[1], row_mean[0])
    scaled = gradient / jnp.sqrt(new_row[:, None] * col_rows / mean_rows[:, None])
    square_part = kernel_sums(jnp.sum(scaled * scaled, axis=1)[:, None], is_small)[:, 0]
    square_total = lax.psum(square_part, "shard")
    clip_factor = jnp.maximum(1.0, jnp.sqrt(square_total / (counts * CO)))
    update_rows = scaled / jnp.where(is_small, clip_factor[1], clip_factor[0])[:, None]
    new_master = master_rows - learn_rate * update_rows
    weights_low = new_master.astype(jnp.bfloat16)
    gathered = lax.all_gather(weights_low, "shard", axis=0, tiled=True)
    inverse = jnp.zeros((NB,), jnp.int32).at[block_order].set(jnp.arange(NB, dtype=jnp.int32))
    natural = jnp.take(gathered.reshape(NB, BLK, CO), inverse, axis=0).reshape(total_rows, CO)
    spatial = natural[: 27 * CI].reshape(27, CI, CO)
    pointwise = natural[27 * CI :]
    hidden_sum = jnp.zeros((FR * HW * HW, CO), jnp.float32)
    for index_tap, view in enumerate(tap_views(next_tiles[0])):
        hidden_sum = hidden_sum + jnp.dot(
            view, spatial[index_tap], preferred_element_type=jnp.float32
        )
    hidden_act = jax.nn.silu(hidden_sum).astype(jnp.bfloat16)
    next_output = jnp.dot(hidden_act, pointwise, preferred_element_type=jnp.float32).astype(
        jnp.bfloat16
    )
    return (update_rows, new_master, new_row, new_col, next_output)


def solution(mesh):
    in_specs = (
        P(),
        P(),
        P(("group", "shard"), None, None, None, None),
        P(("group", "shard"), None),
        P(("group", "shard"), None),
        P(),
        P("shard", None),
        P("shard"),
        P(),
        P(("group", "shard"), None, None, None, None),
    )
    out_specs = (P("shard", None), P("shard", None), P("shard"), P(), P(("group", "shard"), None))
    return jax.shard_map(shards, mesh=mesh, in_specs=in_specs, out_specs=out_specs, check_vma=False)
```

profile of v0, /device:TPU:1, one launch (start us, length us, event | category | flops | bytes accessed | tf_op | source)
XLA Modules:
  0.0 556.7 jit_solution(18183779678937260853)
XLA Ops:
  7.2 1.3 copy.102
  36.3 4.9 gather_fusion
  41.2 3.8 broadcast_select_fusion.1
  46.8 4.5 select_select_fusion
  51.3 150.8 %reduce-scatter.2.cloned.1.call-done = bf16[224,256]{1,0:T(8,128)(2,1)} async-done(((bf16[7168,256]{1,0:T(8,128)(2,1)}), bf16[224,256]{1,0:T(8,128)(2,1)}) %reduce-scatter.2.cloned.1.call-update) | async-done | bytes 114704 | tf_op jit(solution)/shard_map/reduce_scatter | solution.py:72
  202.1 89.2 %all-reduce.2 = f32[224,256]{1,0:T(8,128)S(1)} all-reduce(bf16[224,256]{1,0:T(8,128)(2,1)} %reduce-scatter.2.cloned.1.call-done), channel_id=1, replica_groups=mesh['group'=16,'shard'=32] {'group'}, use_global_device_ids=true, to_apply=%region_1.3 | all-reduce | flops 57344 | bytes 344064 | tf_op jit(solution)/shard_map/psum | solution.py:75
  291.5 5.2 select_reduce_fusion.5
  296.7 1.3 maximum_bitcast_fusion
  298.0 84.7 %all-reduce = (f32[2]{0:T(128)S(1)}, f32[2,256]{1,0:T(2,128)S(1)}) all-reduce(f32[2]{0:T(128)S(1)} %maximum_bitcast_fusion, f32[2,256]{1,0:T(2,128)S(1)} %pad_maximum_fusion), channel_id=1, replica_groups=mesh['group'=16,'shard'=32] {'shard'}, use_global_device_ids=true, to_apply=%region_8.10 | all-reduce | flops 514 | bytes 4112 | tf_op jit(solution)/shard_map/psum | solution.py:86
  383.3 5.7 %broadcast_select_fusion.3 = f32[224]{0:T(256)S(1)} fusion(f32[]{:T(128)} %bitcast.74, f32[]{:T(128)} %bitcast.73, pred[]{:T(512)} %bitcast.65, pred[]{:T(512)} %bitcast.64, pred[]{:T(512)} %bitcast.63, pred[]{:T(512)} %bitcast.62, pred[]{:T(512)} %bitcast.61, pred[]{:T(512)} %bitcast.60, pred[]{:T(512)} %bitcast.59, s32[256]{0:T(256)S(1)} %add_bitcast_fusion), kind=kLoop, calls=%fused_computation.172 | loop fusion | flops 4704 | bytes 1807 | tf_op jit(solution)/shard_map/jit(_where)/select_n | solution.py:90
  389.3 5.2 select_reduce_fusion.3
  394.5 1.3 maximum_bitcast_fusion.1
  395.8 67.4 %psum.31 = f32[2]{0:T(128)S(1)} all-reduce(f32[2]{0:T(128)S(1)} %maximum_bitcast_fusion.1), channel_id=1, replica_groups=mesh['group'=16,'shard'=32] {'shard'}, use_global_device_ids=true, to_apply=%region_12.14 | all-reduce | flops 2 | bytes 16 | tf_op jit(solution)/shard_map/psum | solution.py:93
  463.8 5.7 %broadcast_select_fusion.2 = f32[224]{0:T(256)S(1)} fusion(f32[]{:T(128)} %bitcast.79, f32[]{:T(128)} %bitcast.78, pred[]{:T(512)} %bitcast.65, pred[]{:T(512)} %bitcast.64, pred[]{:T(512)} %bitcast.63, pred[]{:T(512)} %bitcast.62, pred[]{:T(512)} %bitcast.61, pred[]{:T(512)} %bitcast.60, pred[]{:T(512)} %bitcast.59, s32[256]{0:T(256)S(1)} %add_bitcast_fusion), kind=kLoop, calls=%fused_computation.171 | loop fusion | flops 4704 | bytes 1807 | tf_op jit(solution)/shard_map/jit(_where)/select_n | solution.py:95
  470.5 1.5 scatter_custom_fusion
  472.1 1.4 fusion.85
  473.5 2.1 fusion.84
  475.6 53.3 %all-gather.2.cloned.1.call-done = bf16[7168,256]{1,0:T(8,128)(2,1)} async-done(((bf16[224,256]{1,0:T(8,128)(2,1)}), bf16[7168,256]{1,0:T(8,128)(2,1)}) %all-gather.2.cloned.1.call-update) | async-done | bytes 3670032 | tf_op jit(solution)/shard_map/all_gather | solution.py:98
  528.9 4.9 gather_fusion.1
  533.8 2.5 broadcast_select_fusion
  540.1 1.0 convolution_bitcast_fusion.7
  541.1 1.1 convolution_bitcast_fusion.8
  545.9 1.1 fusion.10
  547.0 2.9 convolution_convert_fusion
  (148 shorter events, 38.6 us)
Async XLA Ops:
  7.2 2.3 copy-start
  7.2 194.9 %reduce-scatter.2.cloned.1.call-start = ((), (), s32[]{:S(2)}) async-start(), calls=%async_computation.1 | async-start | bytes 3784704 | tf_op jit(solution)/shard_map/reduce_scatter | solution.py:72
  45.0 1.8 copy-start.28
  45.0 246.5 %copy-start.26 = (f32[224]{0:T(256)S(1)}, f32[224]{0:T(256)}, u32[]{:S(2)}) copy-start(f32[224]{0:T(256)} %param.22) | copy-start | bytes 2692
  45.0 337.7 %copy-start.25 = (f32[2,256]{1,0:T(2,128)S(1)}, f32[2,256]{1,0:T(2,128)}, u32[]{:S(2)}) copy-start(f32[2,256]{1,0:T(2,128)} %param.23) | copy-start | bytes 6148
  45.0 337.7 %copy-start.29 = (f32[2]{0:T(128)S(1)}, f32[2]{0:T(128)}, u32[]{:S(2)}) copy-start(f32[2]{0:T(128)} %constant.126) | copy-start | bytes 28
  45.0 418.2 %copy-start.32 = (f32[2]{0:T(128)S(1)}, f32[2]{0:T(128)}, u32[]{:S(2)}) copy-start(f32[2]{0:T(128)} %constant.129) | copy-start | bytes 28
  45.0 424.5 %copy-start.22 = (f32[224,256]{1,0:T(8,128)S(1)}, f32[224,256]{1,0:T(8,128)}, u32[]{:S(2)}) copy-start(f32[224,256]{1,0:T(8,128)} %param.21) | copy-start | bytes 688132
  45.0 426.9 %copy-start.21 = (bf16[1,4,18,18,256]{4,1,3,2,0:T(4,128)(2,1)S(1)}, bf16[1,4,18,18,256]{4,1,3,2,0:T(4,128)(2,1)}, u32[]{:S(2)}) copy-start(bf16[1,4,18,18,256]{4,1,3,2,0:T(4,128)(2,1)} %param.24) | copy-start | bytes 1990660
  45.0 483.9 %all-gather.2.cloned.1.call-start = ((), (), s32[]{:S(2)}) async-start(), calls=%async_computation.2 | async-start | bytes 3784704 | tf_op jit(solution)/shard_map/all_gather | solution.py:98
  296.7 176.9 %copy-start.24 = (f32[224]{0:T(256)}, f32[224]{0:T(256)S(1)}, u32[]{:S(2)}) copy-start(f32[224]{0:T(256)S(1)} %get-tuple-element.32) | copy-start | bytes 2692
  382.7 90.8 %copy-start.23 = (f32[2,256]{1,0:T(2,128)}, f32[2,256]{1,0:T(2,128)S(1)}, u32[]{:S(2)}) copy-start(f32[2,256]{1,0:T(2,128)S(1)} %multiply_add_fusion) | copy-start | bytes 6148
  537.4 1.4 copy-start.4
  537.4 1.7 copy-start.3
  537.4 2.7 copy-start.2
  537.6 3.5 copy-start.1
  537.8 4.3 copy-start.20
  538.3 4.1 copy-start.19
  538.5 4.1 copy-start.18
  539.0 3.9 copy-start.17
  540.1 3.1 copy-start.16
  542.4 1.3 copy-start.12
  542.6 1.3 copy-start.15
  543.4 1.3 copy-start.10
  (11 other events, 12.7 us)
Sparse Core Ops, SparseCore 0:
  45.2 156.8 reduce-scatter.1
  470.6 58.3 all-gather.1
where the time goes:
time: 557 us
  blocking collectives  241 us (43%)
  waiting for transfers between devices  204 us (37%)
  matrix products  38.5 us (7%)
  other arithmetic  36.8 us (7%)
  local copies, waits for them, and re-layouts  20.3 us (4%)
  between operations  15.6 us (3%)
    reduce_scatter x1, waiting for transfers between devices, shards(): lax.psum_scatter(stored, 'shard', scatter_dimension=0, tiled=True)  151 us
    psum x1, blocking collectives, shards(): gradient = lax.psum(partial_value, 'group')  89.2 us
    psum x1, blocking collectives, shards(): col_total, row_total = lax.psum((col_part, row_part), 'shard')  84.7 us
    psum x1, blocking collectives, shards(): square_total = lax.psum(square_part, 'shard')  67.4 us
    all_gather x1, waiting for transfers between devices, shards(): gathered = lax.all_gather(weights_low, 'shard', axis=0, tiled=True)  53.3 us
    dot_general x28, matrix products, contract_rows(): lax.dot_general(left, right, (((0,), (0,)), ((), ())), preferred_element_...  26.2 us
  transfers between devices with their start and end apart: 2, of which 2 were waited for; matrix products, arithmetic and copies ran while one was open for 2% of the time, Pallas kernels for 0%

commit v1 on v0

v1 whole, which is shorter than its diff:
```python
import jax
import jax.numpy as jnp
from jax import lax
from jax.experimental import pallas as pl
from jax.experimental.pallas import tpu as pltpu
from jax.sharding import PartitionSpec as P

CI = 256
CO = 256
BLK = 32
FR = 2
HW = 16
NB3 = 216
NB = 224
OWN = 7
LARGE = 27.0 * CI
SMALL = 1.0 * CI

learn_rate = 0.002
decay_power = 0.8

MESH = pl.DeviceIdType.MESH


def silu_slope(values):
    sigma = jax.nn.sigmoid(values)
    return sigma * (1.0 + values * (1.0 - sigma))


def tap_views(frames):
    views = []
    for frame_off in range(3):
        for row_off in range(3):
            for col_off in range(3):
                window = frames[
                    frame_off : frame_off + FR, row_off : row_off + HW, col_off : col_off + HW, :
                ]
                views.append(window.reshape(FR * HW * HW, CI))
    return views


def contract_rows(left, right):
    return lax.dot_general(
        left, right, (((0,), (0,)), ((), ())), preferred_element_type=jnp.float32
    )


def step_kernel(
    term,
    aux,
    row_in,
    master,
    update,
    new_master,
    new_row,
    new_col,
    weights,
    core_in,
    y_sum,
    y_half,
    y_full,
    x_sum,
    x_half,
    x_full,
    z_sum,
    z_in,
    h_in,
    grad,
    stat_own,
    stat_core,
    stat_y,
    stat_z,
    send_sem,
    recv_sem,
):
    group = lax.axis_index("group")
    shard = lax.axis_index("shard")
    x = group // 4
    zh = group % 4
    c = shard % 2
    y = (shard // 2) % 4
    zl = shard // 8

    def dev_core():
        return (group, shard + 1 - 2 * c)

    def dev_y(d):
        return (group, zl * 8 + ((y + d) % 4) * 2 + c)

    def dev_z(d):
        return (group, ((zl + d) % 4) * 8 + y * 2 + c)

    def dev_x(d):
        return (((x + d) % 4) * 4 + zh, shard)

    def dev_h(d):
        return (x * 4 + (zh + d) % 4, shard)

    partners = [dev_core()]
    partners += [dev_y(d) for d in (1, 2, 3)]
    partners += [dev_x(d) for d in (1, 3)]
    partners += [dev_z(d) for d in (1, 2, 3)]
    partners += [dev_h(d) for d in (1, 2, 3)]
    barrier = pltpu.get_barrier_semaphore()
    for partner in partners:
        pl.semaphore_signal(barrier, inc=1, device_id=partner, device_id_type=MESH)
    pl.semaphore_wait(barrier, len(partners))

    started = []

    def send(src, dst, device):
        slot = len(started)
        copy = pltpu.make_async_remote_copy(
            src_ref=src,
            dst_ref=dst,
            send_sem=send_sem.at[slot],
            recv_sem=recv_sem.at[slot],
            device_id=device,
            device_id_type=MESH,
        )
        copy.start()
        started.append(copy)
        return copy

    f32 = jnp.float32
    bf16 = jnp.bfloat16

    def add_into(dst, count, reads):
        @pl.loop(0, count)
        def _(step):
            total = reads[0](step).astype(f32)
            for read in reads[1:]:
                total = total + read(step).astype(f32)
            dst(step, total.astype(bf16))

    core_copies = {}
    for d in (2, 1, 3, 0):
        j = (y + d) % 4
        core_copies[d] = send(term.at[1 - c, j], core_in.at[j], dev_core())

    def y_part(d, start, count, more=()):
        j = (y + d) % 4

        def put(step, value):
            y_sum[d, start + step // 4, step % 4] = value

        reads = [
            lambda step: term[c, j, start + step // 4, step % 4],
            lambda step: core_in[j, start + step // 4, step % 4],
        ]
        for slot in more:
            reads.append(lambda step, slot=slot: y_half[slot, step // 4, step % 4])
        add_into(put, 4 * count, reads)

    core_copies[2].wait_recv()
    y_part(2, 0, 2)
    half_0 = send(y_sum.at[2, pl.ds(0, 2)], y_half.at[0], dev_y(1))
    y_part(2, 2, 2)
    half_1 = send(y_sum.at[2, pl.ds(2, 2)], y_half.at[1], dev_y(3))
    core_copies[1].wait_recv()
    y_part(1, 2, 2)
    full_0b = send(y_sum.at[1, pl.ds(2, 2)], y_full.at[0, pl.ds(2, 2)], dev_y(1))
    core_copies[3].wait_recv()
    y_part(3, 0, 2)
    full_1a = send(y_sum.at[3, pl.ds(0, 2)], y_full.at[1, pl.ds(0, 2)], dev_y(3))
    half_0.wait_recv()
    y_part(1, 0, 2, more=(0,))
    full_0a = send(y_sum.at[1, pl.ds(0, 2)], y_full.at[0, pl.ds(0, 2)], dev_y(1))
    half_1.wait_recv()
    y_part(3, 2, 2, more=(1,))
    full_1b = send(y_sum.at[3, pl.ds(2, 2)], y_full.at[1, pl.ds(2, 2)], dev_y(3))
    core_copies[0].wait_recv()
    for copy in (full_0b, full_1a, full_0a, full_1b):
        copy.wait_recv()

    def x_part(d, start, count, more=()):
        q = (x + d) % 4

        def put(step, value):
            x_sum[d, start + step] = value

        reads = [
            lambda step: term[c, y, q, start + step],
            lambda step: core_in[y, q, start + step],
            lambda step: y_full[0, q, start + step],
            lambda step: y_full[1, q, start + step],
        ]
        for slot in more:
            reads.append(lambda step, slot=slot: x_half[slot, step])
        add_into(put, count, reads)

    x_part(2, 0, 2)
    half_0 = send(x_sum.at[2, pl.ds(0, 2)], x_half.at[0], dev_x(1))
    x_part(2, 2, 2)
    half_1 = send(x_sum.at[2, pl.ds(2, 2)], x_half.at[1], dev_x(3))
    x_part(1, 2, 2)
    full_0b = send(x_sum.at[1, pl.ds(2, 2)], x_full.at[0, pl.ds(2, 2)], dev_x(1))
    x_part(3, 0, 2)
    full_1a = send(x_sum.at[3, pl.ds(0, 2)], x_full.at[1, pl.ds(0, 2)], dev_x(3))
    half_0.wait_recv()
    x_part(1, 0, 2, more=(0,))
    full_0a = send(x_sum.at[1, pl.ds(0, 2)], x_full.at[0, pl.ds(0, 2)], dev_x(1))
    half_1.wait_recv()
    x_part(3, 2, 2, more=(1,))
    full_1b = send(x_sum.at[3, pl.ds(2, 2)], x_full.at[1, pl.ds(2, 2)], dev_x(3))
    x_part(0, 0, 4)
    for copy in (full_0b, full_1a, full_0a, full_1b):
        copy.wait_recv()

    z_copies = []
    for d in (3, 2, 1, 0):
        z = (zl + d) % 4
        z_sum[d] = (
            x_sum[0, z].astype(f32) + x_full[0, z].astype(f32) + x_full[1, z].astype(f32)
        ).astype(bf16)
        if d:
            z_copies.append(send(z_sum.at[d], z_in.at[d - 1], dev_z(d)))
    for copy in z_copies:
        copy.wait_recv()
    h_in[zh] = (
        (z_sum[0].astype(f32) + z_in[0].astype(f32))
        + (z_in[1].astype(f32) + z_in[2].astype(f32))
    ).astype(bf16)

    h_copies = [send(h_in.at[zh], h_in.at[zh], dev_h(d)) for d in (2, 1, 3)]
    for copy in h_copies:
        copy.wait_recv()
    grad[x] = (
        (h_in[0].astype(f32) + h_in[1].astype(f32)) + (h_in[2].astype(f32) + h_in[3].astype(f32))
    ).astype(bf16)

    left = (x + 3) % 4
    right = (x + 1) % 4
    to_right = send(grad.at[x], grad.at[x], dev_x(1))
    to_left = send(grad.at[x], grad.at[x], dev_x(3))
    to_right.wait_recv()
    on_right = send(grad.at[left, pl.ds(0, 4)], grad.at[left, pl.ds(0, 4)], dev_x(1))
    to_left.wait_recv()
    on_left = send(grad.at[right, pl.ds(4, 3)], grad.at[right, pl.ds(4, 3)], dev_x(3))
    on_right.wait_recv()
    on_left.wait_recv()

    decay = aux[0:1, :]
    decay_row = aux[0:1, 0:1]
    zero = jnp.zeros((1, 128), f32)
    zero_row = jnp.zeros((1, 1), f32)
    cols = [[zero, zero], [zero, zero]]
    mixed = [[zero, zero], [zero, zero]]
    rows = [zero_row, zero_row]
    for i in range(OWN):
        small = aux[8 + i : 9 + i, 0:128]
        is_kernel = (1.0 - small, small)
        for half in range(2):
            span = slice(16 * half, 16 * half + 16)
            squares = []
            for side in range(2):
                value = grad[2 * half + side, i].astype(f32)
                squares.append(value * value)
            mean = jnp.sum(squares[0] + squares[1], axis=1, keepdims=True) * (1.0 / CO)
            moment = decay_row * row_in[i, span, :] + (1.0 - decay_row) * mean
            new_row[i, span, :] = moment
            inverse = 1.0 / moment
            row_sum = jnp.sum(moment, axis=0, keepdims=True)
            for k in range(2):
                rows[k] = rows[k] + is_kernel[k][:, 0:1] * row_sum
            for side in range(2):
                plain = jnp.sum(squares[side], axis=0, keepdims=True)
                weighted = jnp.sum(squares[side] * inverse, axis=0, keepdims=True)
                for k in range(2):
                    cols[k][side] = cols[k][side] + is_kernel[k] * plain
                    mixed[k][side] = mixed[k][side] + is_kernel[k] * weighted
    for side in range(2):
        lanes = slice(128 * side, 128 * side + 128)
        for k in range(2):
            stat_own[k : k + 1, lanes] = cols[k][side]
            stat_own[2 + k : 3 + k, lanes] = mixed[k][side]
            stat_own[4 + k : 5 + k, lanes] = jnp.broadcast_to(rows[k], (1, 128))
        stat_own[6:8, lanes] = jnp.zeros((2, 128), f32)

    send(stat_own, stat_core, dev_core()).wait_recv()
    stat_y[y] = stat_own[...] + stat_core[...]
    y_copies = [send(stat_y.at[y], stat_y.at[y], dev_y(d)) for d in (2, 1, 3)]
    for copy in y_copies:
        copy.wait_recv()
    stat_z[zl] = (stat_y[0] + stat_y[1]) + (stat_y[2] + stat_y[3])
    z_copies = [send(stat_z.at[zl], stat_z.at[zl], dev_z(d)) for d in (3, 2, 1)]
    for copy in z_copies:
        copy.wait_recv()
    total = (stat_z[0] + stat_z[1]) + (stat_z[2] + stat_z[3])

    factors = []
    for k, rows_k in ((0, LARGE), (1, SMALL)):
        column = decay * aux[1 + k : 2 + k, :] + (1.0 - decay) * total[k : k + 1, :] / rows_k
        new_col[k : k + 1, :] = column
        row_mean = total[4 + k : 5 + k, 0:1] / rows_k
        square = row_mean * jnp.sum(total[2 + k : 3 + k, :] / column, axis=1, keepdims=True)
        clip = jnp.maximum(1.0, jnp.sqrt(square / (rows_k * CO)))
        factors.append(1.0 / (jnp.sqrt(column / row_mean) * clip))
    new_col[2:8, :] = jnp.zeros((6, 256), f32)

    for i in range(OWN):
        small = aux[8 + i : 9 + i, :]
        factor = (1.0 - small) * factors[0] + small * factors[1]
        for half in range(2):
            span = slice(16 * half, 16 * half + 16)
            scale = 1.0 / jnp.sqrt(new_row[i, span, :])
            for side in range(2):
                lanes = slice(128 * side, 128 * side + 128)
                value = grad[2 * half + side, i].astype(f32)
                change = value * scale * factor[:, lanes]
                update[i, span, lanes] = change
                fresh = master[i, span, lanes] - learn_rate * change
                new_master[i, span, lanes] = fresh
                quarter = 2 * half + side

                @pl.when(x == quarter)
                def _(fresh=fresh, quarter=quarter, i=i):
                    weights[c, y, quarter, zl, i] = fresh.astype(bf16)

    z_copies = [
        send(weights.at[c, y, x, zl], weights.at[c, y, x, zl], dev_z(d)) for d in (3, 2, 1)
    ]
    for copy in z_copies:
        copy.wait_recv()
    to_right = send(weights.at[c, y, x], weights.at[c, y, x], dev_x(1))
    to_left = send(weights.at[c, y, x], weights.at[c, y, x], dev_x(3))
    to_right.wait_recv()
    low, high = pl.ds(0, 2), pl.ds(2, 2)
    on_right = send(weights.at[c, y, left, low], weights.at[c, y, left, low], dev_x(1))
    to_left.wait_recv()
    on_left = send(weights.at[c, y, right, high], weights.at[c, y, right, high], dev_x(3))
    on_right.wait_recv()
    on_left.wait_recv()
    below = (y + 3) % 4
    above = (y + 1) % 4
    across = (y + 2) % 4
    to_above = send(weights.at[c, y], weights.at[c, y], dev_y(1))
    to_below = send(weights.at[c, y], weights.at[c, y], dev_y(3))
    cores = [send(weights.at[c, y], weights.at[c, y], dev_core())]
    to_above.wait_recv()
    on_above = send(weights.at[c, below, low], weights.at[c, below, low], dev_y(1))
    cores.append(send(weights.at[c, below], weights.at[c, below], dev_core()))
    to_below.wait_recv()
    on_below = send(weights.at[c, above, high], weights.at[c, above, high], dev_y(3))
    cores.append(send(weights.at[c, above], weights.at[c, above], dev_core()))
    on_above.wait_recv()
    cores.append(send(weights.at[c, across, low], weights.at[c, across, low], dev_core()))
    on_below.wait_recv()
    cores.append(send(weights.at[c, across, high], weights.at[c, across, high], dev_core()))
    for copy in cores:
        copy.wait_recv()
    assert len(started) == N_COPIES
    for copy in started:
        copy.wait_send()


N_COPIES = 49


def optimizer_step(term, aux, row_in, master):
    f32 = jnp.float32
    bf16 = jnp.bfloat16
    tile = (OWN, 16, 128)
    vmem = pl.BlockSpec(memory_space=pltpu.VMEM)
    return pl.pallas_call(
        step_kernel,
        name="optimizer_step",
        out_shape=(
            jax.ShapeDtypeStruct((OWN, 32, 256), f32),
            jax.ShapeDtypeStruct((OWN, 32, 256), f32),
            jax.ShapeDtypeStruct((OWN, 32, 1), f32),
            jax.ShapeDtypeStruct((8, 256), f32),
            jax.ShapeDtypeStruct((2, 4, 4, 4) + tile, bf16),
        ),
        in_specs=[vmem] * 4,
        out_specs=[vmem] * 5,
        scratch_shapes=[
            pltpu.VMEM((4, 4, 4) + tile, bf16),
            pltpu.VMEM((4, 4, 4) + tile, bf16),
            pltpu.VMEM((2, 2, 4) + tile, bf16),
            pltpu.VMEM((2, 4, 4) + tile, bf16),
            pltpu.VMEM((4, 4) + tile, bf16),
            pltpu.VMEM((2, 2) + tile, bf16),
            pltpu.VMEM((2, 4) + tile, bf16),
            pltpu.VMEM((4,) + tile, bf16),
            pltpu.VMEM((3,) + tile, bf16),
            pltpu.VMEM((4,) + tile, bf16),
            pltpu.VMEM((4,) + tile, bf16),
            pltpu.VMEM((8, 256), f32),
            pltpu.VMEM((8, 256), f32),
            pltpu.VMEM((4, 8, 256), f32),
            pltpu.VMEM((4, 8, 256), f32),
            pltpu.SemaphoreType.DMA((N_COPIES,)),
            pltpu.SemaphoreType.DMA((N_COPIES,)),
        ],
        compiler_params=pltpu.CompilerParams(collective_id=0, has_side_effects=True),
    )(term, aux, row_in, master)


def shards(
    step_count,
    block_order,
    saved_tiles,
    pre_act,
    grad_output,
    pointwise_live,
    master_rows,
    row_moment,
    col_moment,
    next_tiles,
):
    pre_float = pre_act.astype(jnp.float32)
    activation = jax.nn.silu(pre_float).astype(jnp.bfloat16)
    grad_act = lax.dot_general(
        grad_output, pointwise_live, (((1,), (1,)), ((), ())), preferred_element_type=jnp.float32
    )
    grad_pre = (grad_act * silu_slope(pre_float)).astype(jnp.bfloat16)
    pieces = [contract_rows(view, grad_pre) for view in tap_views(saved_tiles[0])]
    pieces.append(contract_rows(activation, grad_output))
    own_term = jnp.concatenate(pieces, axis=0).astype(jnp.bfloat16)
    total_rows = NB * BLK
    order = block_order.reshape(4, 4, 2, OWN).transpose(2, 1, 0, 3)
    quarters = jnp.arange(4, dtype=jnp.int32)[None, None, :, None, None]
    source = order[:, :, None] * 4 + quarters
    tiles = own_term.reshape(NB, 2, 16, 2, 128).transpose(0, 1, 3, 2, 4).reshape(NB * 4, 16, 128)
    term = jnp.take(tiles, source.reshape(-1), axis=0).reshape(2, 4, 4, 4, OWN, 16, 128)

    owner = lax.axis_index("shard")
    own_blocks = lax.dynamic_slice_in_dim(block_order, owner * OWN, OWN)
    is_small = (own_blocks >= NB3).astype(jnp.float32)
    decay_rate = 1.0 - step_count.astype(jnp.float32)[0] ** (-decay_power)
    aux = jnp.concatenate(
        [
            jnp.broadcast_to(decay_rate, (1, CO)),
            col_moment,
            jnp.zeros((5, CO), jnp.float32),
            jnp.broadcast_to(is_small[:, None], (OWN, CO)),
            jnp.zeros((1, CO), jnp.float32),
        ],
        axis=0,
    )
    update, new_master, new_row, new_col, gathered = optimizer_step(
        term, aux, row_moment.reshape(OWN, BLK, 1), master_rows.reshape(OWN, BLK, CO)
    )
    position = jnp.zeros((NB,), jnp.int32).at[order.reshape(-1)].set(jnp.arange(NB, dtype=jnp.int32))
    outer, inner = position // 28, position % 28
    place = outer[:, None] * 112 + jnp.arange(4, dtype=jnp.int32)[None, :] * 28 + inner[:, None]
    natural = jnp.take(gathered.reshape(NB * 4, 16, 128), place.reshape(-1), axis=0)
    natural = natural.reshape(NB, 2, 2, 16, 128).transpose(0, 1, 3, 2, 4).reshape(total_rows, CO)
    spatial = natural[: 27 * CI].reshape(27, CI, CO)
    pointwise = natural[27 * CI :]
    hidden_sum = jnp.zeros((FR * HW * HW, CO), jnp.float32)
    for index_tap, view in enumerate(tap_views(next_tiles[0])):
        hidden_sum = hidden_sum + jnp.dot(
            view, spatial[index_tap], preferred_element_type=jnp.float32
        )
    hidden_act = jax.nn.silu(hidden_sum).astype(jnp.bfloat16)
    next_output = jnp.dot(hidden_act, pointwise, preferred_element_type=jnp.float32).astype(
        jnp.bfloat16
    )
    return (
        update.reshape(master_rows.shape),
        new_master.reshape(master_rows.shape),
        new_row.reshape(row_moment.shape),
        new_col[:2],
        next_output,
    )


def solution(mesh):
    in_specs = (
        P(),
        P(),
        P(("group", "shard"), None, None, None, None),
        P(("group", "shard"), None),
        P(("group", "shard"), None),
        P(),
        P("shard", None),
        P("shard"),
        P(),
        P(("group", "shard"), None, None, None, None),
    )
    out_specs = (P("shard", None), P("shard", None), P("shard"), P(), P(("group", "shard"), None))
    return jax.shard_map(shards, mesh=mesh, in_specs=in_specs, out_specs=out_specs, check_vma=False)
```

time: 557 us -> 199 us (0.36)
  blocking collectives: 241 us -> 0 us
  waiting for transfers between devices: 204 us -> 0 us
  Pallas kernels: 0 us -> 105 us
  other arithmetic: 36.8 us -> 12.2 us
  local copies, waits for them, and re-layouts: 20.3 us -> 39.5 us
  between operations: 15.6 us -> 1.99 us
    psum x3 -> x0, blocking collectives: 241 us -> none  [the longest x1 89.2 us: shards(): gradient = lax.psum(partial_value, 'group')]
    reduce_scatter x1 -> x0, waiting for transfers between devices: 151 us -> none  [shards(): lax.psum_scatter(stored, 'shard', scatter_dimension=0, tiled=True)]
    pallas_call x0 -> x1, Pallas kernels: none -> 105 us  [optimizer_step(): pl.pallas_call(step_kernel, name='optimizer_step', out_shape=(jax.ShapeDt...]
    all_gather x1 -> x0, waiting for transfers between devices: 53.3 us -> none  [shards(): gathered = lax.all_gather(weights_low, 'shard', axis=0, tiled=True)]
    select_n x7 -> x5, other arithmetic: 22.2 us -> 11 us  [the longest x2 6.09 us: shards(): jnp.take(tiles, source.reshape(-1), axis=0)]
    convert_element_type x0 -> x2, local copies, waits for them, and re-layouts: none -> 11.1 us  [shards(): own_term = jnp.concatenate(pieces, axis=0).astype(jnp.bfloat16)]
    reduce_sum x4 -> x0, other arithmetic: 10.8 us -> none  [the longest x3 10.5 us: kernel_sums(): large_part = jnp.sum(jnp.where(is_small[:, None], 0.0, values), axis=0)]
  transfers between devices with their start and end apart: 2 -> 0, of which waited for: 2 -> 0; matrix products, arithmetic and copies ran while one was open for 2% -> 0% of each run, Pallas kernels for 0% -> 0%
where the time goes in v1:
time: 199 us; the launch traced here: 198 us
  Pallas kernels  105 us (53%)
  matrix products  39.6 us (20%)
  local copies, waits for them, and re-layouts  39.5 us (20%)
  other arithmetic  12.2 us (6%)
  between operations  1.99 us (1%)
    pallas_call x1, Pallas kernels, optimizer_step(): pl.pallas_call(step_kernel, name='optimizer_step', out_shape=(jax.ShapeDt...  105 us
    dot_general x28, matrix products, contract_rows(): lax.dot_general(left, right, (((0,), (0,)), ((), ())), preferred_element_...  26.2 us
    convert_element_type x2, local copies, waits for them, and re-layouts, shards(): own_term = jnp.concatenate(pieces, axis=0).astype(jnp.bfloat16)  11.1 us
    dot_general x26, matrix products, shards(): jnp.dot(view, spatial[index_tap], preferred_element_type=jnp.float32)  9.19 us
    select_n x2, other arithmetic, shards(): jnp.take(tiles, source.reshape(-1), axis=0)  6.09 us
    gather x1, local copies, waits for them, and re-layouts, shards(): jnp.take(tiles, source.reshape(-1), axis=0)  5.33 us
    gather x1, local copies, waits for them, and re-layouts, shards(): jnp.take(gathered.reshape(NB * 4, 16, 128), place.reshape(-1), axis=0)  5.33 us
    select_n x2, other arithmetic, shards(): jnp.take(gathered.reshape(NB * 4, 16, 128), place.reshape(-1), axis=0)  4.87 us

profile of v1, /device:TPU:1, one launch (start us, length us, event | category | flops | bytes accessed | tf_op | source)
XLA Modules:
  0.0 198.3 jit_solution(3051230264298165102)
XLA Ops:
  1.6 1.3 fusion.11
  5.2 0.9 fusion.18
  16.1 0.9 fusion.40
  24.5 0.9 fusion.58
  29.2 1.0 fusion.12
  30.2 6.3 %convert_element_type.29 = bf16[224,2,16,2,128]{4,3,2,1,0:T(2,128)(2,1)} reshape(bf16[7168,256]{1,0:T(8,128)(2,1)} %fusion.12) | data formatting | bytes 7340032 | tf_op jit(solution)/shard_map/convert_element_type | solution.py:420
  36.5 4.8 %copy.137 = bf16[224,2,16,2,128]{4,2,3,1,0:T(8,128)(2,1)} copy(bf16[224,2,16,2,128]{4,3,2,1,0:T(2,128)(2,1)} %convert_element_type.29) | data formatting | bytes 7340032 | tf_op jit(solution)/shard_map/convert_element_type | solution.py:420
  41.6 1.5 scatter_custom_fusion
  43.6 5.3 %gather_fusion = bf16[896,16,128]{2,1,0:T(8,128)(2,1)} fusion(bf16[896,16,128]{2,1,0:T(8,128)(2,1)} %bitcast.461, s32[1024]{0:T(1024)S(1)} %get-tuple-element.101), kind=kCustom, calls=%fused_computation.clone | custom fusion | bytes 7343616 | tf_op jit(solution)/shard_map/jit(_take)/gather | solution.py:426
  49.0 6.1 %broadcast_select_fusion.1 = bf16[896,16,128]{2,1,0:T(8,128)(2,1)} fusion(bf16[896,16,128]{2,1,0:T(8,128)(2,1)} %gather_fusion, pred[896]{0:T(1024)(128)(4,1)S(1)} %compare_and_fusion.1), kind=kLoop, calls=%fused_computation.4 | loop fusion | flops 1835008 | bytes 7340928 | tf_op jit(solution)/shard_map/jit(_take)/select_n | solution.py:426
  56.0 1.2 concatenate.8.aux
  58.1 104.9 %optimizer_step.1 = (f32[7,32,256]{2,1,0:T(8,128)}, f32[7,32,256]{2,1,0:T(8,128)}, f32[7,32,1]{2,1,0:T(8,128)}, f32[8,256]{1,0:T(8,128)}, bf16[2,4,4,4,7,16,128]{6,5,4,3,2,1,0:T(8,128)(2,1)}) custom-call(bf16[2,4,4,4,7,16,128]{6,5,4,3,2,1,0:T(8,128)(2,1)} %bitcast.464, f32[16,256]{1,0:T(8,128)} %concatenate.8.aux, f32[7,32,1]{2,1,0:T(8,128)} %reshape.420.row_in, ...), custom_call_target="tpu_custom_call" | custom-call | tf_op jit(solution)/shard_map/optimizer_step/pallas_call | solution.py:365
  163.0 5.3 %gather_fusion.1 = bf16[896,16,128]{2,1,0:T(8,128)(2,1)} fusion(bf16[896,16,128]{2,1,0:T(8,128)(2,1)} %bitcast.465, s32[1024]{0:T(1024)S(1)} %get-tuple-element.100), kind=kCustom, calls=%fused_computation.1.clone | custom fusion | bytes 7343616 | tf_op jit(solution)/shard_map/jit(_take)/gather | solution.py:448
  168.3 4.9 %broadcast_select_fusion = bf16[896,16,128]{2,1,0:T(8,128)(2,1)S(1)} fusion(bf16[896,16,128]{2,1,0:T(8,128)(2,1)} %gather_fusion.1, pred[896]{0:T(1024)(128)(4,1)S(1)} %compare_and_fusion), kind=kLoop, calls=%fused_computation.3 | loop fusion | flops 1835008 | bytes 7340928 | tf_op jit(solution)/shard_map/jit(_take)/select_n | solution.py:448
  176.8 1.3 fusion.142
  181.7 1.1 fusion.10
  184.9 1.1 convolution_bitcast_fusion.7
  186.1 1.1 convolution_bitcast_fusion.8
  187.3 1.0 convolution_bitcast_fusion
  189.2 2.9 %convolution_convert_fusion = bf16[512,256]{1,0:T(8,128)(2,1)} fusion(f32[512,256]{1,0:T(8,128)} %convolution_bitcast_fusion, f32[512,256]{1,0:T(8,128)S(1)} %convolution_bitcast_fusion.1, f32[512,256]{1,0:T(8,128)S(1)} %convolution_bitcast_fusion.2, f32[512,256]{1,0:T(8,128)S(1)} %convolution_bitcast_fusion.3, ...), kind=kOutput, calls=%fused_computation.43 | convolution fusion | flops 136314880 | bytes 6029312 | tf_op jit(solution)/shard_map/dot_general | solution.py:458
  192.1 1.0 reduce
  193.7 1.3 slice.335
  195.0 1.6 copy.401
  196.6 1.6 copy.402
  (121 shorter events, 36.8 us)
Async XLA Ops:
  0.6 1.0 copy-start
  0.6 2.3 %copy-start.2 = (bf16[1,4,18,18,256]{4,1,3,2,0:T(4,128)(2,1)S(1)}, bf16[1,4,18,18,256]{4,1,3,2,0:T(4,128)(2,1)}, u32[]{:S(2)}) copy-start(bf16[1,4,18,18,256]{4,1,3,2,0:T(4,128)(2,1)} %param.14) | copy-start | bytes 1990660
  18.9 10.3 %copy-start.7 = (bf16[512,256]{1,0:T(8,128)(2,1)S(1)}, bf16[512,256]{1,0:T(8,128)(2,1)}, u32[]{:S(2)}) copy-start(bf16[512,256]{1,0:T(8,128)(2,1)} %param.15) | copy-start | bytes 786436
  36.5 4.8 %copy-start.6 = (s32[224]{0:T(256)S(1)}, s32[224]{0:T(256)}, u32[]{:S(2)}) copy-start(s32[224]{0:T(256)} %param.13) | copy-start | bytes 2692
  49.0 7.0 %copy-start.4 = (f32[2,256]{1,0:T(2,128)S(1)}, f32[2,256]{1,0:T(2,128)}, u32[]{:S(2)}) copy-start(f32[2,256]{1,0:T(2,128)} %param.20) | copy-start | bytes 6148
  49.0 8.2 %copy-start.5 = (f32[224]{0:T(256)S(1)}, f32[224]{0:T(256)}, u32[]{:S(2)}) copy-start(f32[224]{0:T(256)} %param.19) | copy-start | bytes 2692
  168.3 5.2 %copy-start.3 = (bf16[1,4,18,18,256]{4,1,3,2,0:T(4,128)(2,1)S(1)}, bf16[1,4,18,18,256]{4,1,3,2,0:T(4,128)(2,1)}, u32[]{:S(2)}) copy-start(bf16[1,4,18,18,256]{4,1,3,2,0:T(4,128)(2,1)} %param.21) | copy-start | bytes 1990660
  188.4 9.8 %copy-start.1 = (bf16[512,256]{1,0:T(8,128)(2,1)S(1)}, bf16[512,256]{1,0:T(8,128)(2,1)}, u32[]{:S(2)}) copy-start(bf16[512,256]{1,0:T(8,128)(2,1)} %param.16) | copy-start | bytes 786436

commit v2 on v1

--- a/solution.py
+++ b/solution.py
@@ -20,29 +20,6 @@
 decay_power = 0.8
 
 MESH = pl.DeviceIdType.MESH
-
-
-def silu_slope(values):
-    sigma = jax.nn.sigmoid(values)
-    return sigma * (1.0 + values * (1.0 - sigma))
-
-
-def tap_views(frames):
-    views = []
-    for frame_off in range(3):
-        for row_off in range(3):
-            for col_off in range(3):
-                window = frames[
-                    frame_off : frame_off + FR, row_off : row_off + HW, col_off : col_off + HW, :
-                ]
-                views.append(window.reshape(FR * HW * HW, CI))
-    return views
-
-
-def contract_rows(left, right):
-    return lax.dot_general(
-        left, right, (((0,), (0,)), ((), ())), preferred_element_type=jnp.float32
-    )
 
 
 def step_kernel(
@@ -397,6 +374,142 @@
     )(term, aux, row_in, master)
 
 
+def shift_columns(tiles, shifted):
+    @pl.loop(0, (FR + 2) * (HW + 2))
+    def _(step):
+        frame, line = step // (HW + 2), step % (HW + 2)
+        cells = tiles[0, frame, line].astype(jnp.float32)
+        for off in range(3):
+            shifted[off, frame, line] = cells[off : off + HW].astype(jnp.bfloat16)
+
+
+def each_stored_block(order, visit):
+    @pl.loop(0, 32)
+    def _(owner):
+        outer = (owner % 2) * 4 + (owner // 2) % 4
+        for i in range(OWN):
+            visit(order[owner * OWN + i], outer, (owner // 8) * OWN + i)
+
+
+def backward_kernel(order, tiles, pre, grad_out, live, term, shifted, left, right, act, outer, inner):
+    f32 = jnp.float32
+    bf16 = jnp.bfloat16
+
+    def note(block, outer_place, inner_place):
+        outer[block] = outer_place
+        inner[block] = inner_place
+
+    each_stored_block(order, note)
+    shift_columns(tiles, shifted)
+    for part in range(4):
+        rows = slice(128 * part, 128 * part + 128)
+        values = pre[rows, :].astype(f32)
+        sigma = jax.nn.sigmoid(values)
+        act[rows, :] = (values * sigma).astype(bf16)
+        cotangent = grad_out[rows, :]
+        grad_act = lax.dot_general(
+            cotangent, live[...], (((1,), (1,)), ((), ())), preferred_element_type=f32
+        )
+        grad_pre = grad_act * (sigma * (1.0 + values * (1.0 - sigma)))
+        left[:, rows] = grad_pre.T.astype(bf16)
+        right[:, rows] = cotangent.astype(f32).T.astype(bf16)
+
+    def emit(first_block, product):
+        result = product.T.astype(bf16)
+        for j in range(8):
+            block = first_block + j
+            for q in range(4):
+                row = 32 * j + 16 * (q // 2)
+                lane = 128 * (q % 2)
+                term[outer[block], q, inner[block]] = result[row : row + 16, lane : lane + 128]
+
+    @pl.loop(0, 9)
+    def _(spot):
+        down, across = spot // 3, spot % 3
+        for frame in range(3):
+            window = shifted[across, frame : frame + FR, pl.ds(down, HW)].reshape(FR * HW * HW, CI)
+            product = jnp.dot(left[...], window, preferred_element_type=f32)
+            emit(8 * (9 * frame + spot), product)
+
+    emit(NB3, jnp.dot(right[...], act[...], preferred_element_type=f32))
+
+
+def backward(block_order, saved_tiles, pre_act, grad_output, pointwise_live):
+    bf16 = jnp.bfloat16
+    vmem = pl.BlockSpec(memory_space=pltpu.VMEM)
+    smem = pl.BlockSpec(memory_space=pltpu.SMEM)
+    return pl.pallas_call(
+        backward_kernel,
+        name="backward",
+        out_shape=jax.ShapeDtypeStruct((8, 4, 28, 16, 128), bf16),
+        in_specs=[smem] + [vmem] * 4,
+        out_specs=vmem,
+        scratch_shapes=[
+            pltpu.VMEM((3, FR + 2, HW + 2, HW, CI), bf16),
+            pltpu.VMEM((CO, FR * HW * HW), bf16),
+            pltpu.VMEM((CO, FR * HW * HW), bf16),
+            pltpu.VMEM((FR * HW * HW, CO), bf16),
+            pltpu.SMEM((NB,), jnp.int32),
+            pltpu.SMEM((NB,), jnp.int32),
+        ],
+    )(block_order, saved_tiles, pre_act, grad_output, pointwise_live)
+
+
+def forward_kernel(
+    order, tiles, gathered, update_in, master_in, output, update, master, shifted, kernels, hidden
+):
+    f32 = jnp.float32
+    update[...] = update_in[...]
+    master[...] = master_in[...]
+    shift_columns(tiles, shifted)
+
+    def place(block, outer, inner):
+        for q in range(4):
+            lane = 128 * (q % 2)
+            kernels[block, q // 2, :, lane : lane + 128] = gathered[outer, q, inner]
+
+    each_stored_block(order, place)
+    hidden[...] = jnp.zeros_like(hidden)
+
+    @pl.loop(0, 9)
+    def _(spot):
+        down, across = spot // 3, spot % 3
+        for frame in range(3):
+            window = shifted[across, frame : frame + FR, pl.ds(down, HW)].reshape(FR * HW * HW, CI)
+            matrix = kernels[pl.ds(8 * (9 * frame + spot), 8)].reshape(CI, CO)
+            hidden[...] += jnp.dot(window, matrix, preferred_element_type=f32)
+
+    pointwise = kernels[NB3:NB].reshape(CO, CO)
+    for part in range(4):
+        rows = slice(128 * part, 128 * part + 128)
+        values = hidden[rows, :]
+        acted = (values * jax.nn.sigmoid(values)).astype(jnp.bfloat16)
+        output[rows, :] = jnp.dot(acted, pointwise, preferred_element_type=f32).astype(jnp.bfloat16)
+
+
+def forward(block_order, next_tiles, gathered, update, master):
+    bf16 = jnp.bfloat16
+    f32 = jnp.float32
+    vmem = pl.BlockSpec(memory_space=pltpu.VMEM)
+    smem = pl.BlockSpec(memory_space=pltpu.SMEM)
+    return pl.pallas_call(
+        forward_kernel,
+        name="forward",
+        out_shape=(
+            jax.ShapeDtypeStruct((FR * HW * HW, CO), bf16),
+            jax.ShapeDtypeStruct(update.shape, f32),
+            jax.ShapeDtypeStruct(master.shape, f32),
+        ),
+        in_specs=[smem] + [vmem] * 4,
+        out_specs=[vmem] * 3,
+        scratch_shapes=[
+            pltpu.VMEM((3, FR + 2, HW + 2, HW, CI), bf16),
+            pltpu.VMEM((NB, 2, 16, CO), bf16),
+            pltpu.VMEM((FR * HW * HW, CO), f32),
+        ],
+    )(block_order, next_tiles, gathered, update, master)
+
+
 def shards(
     step_count,
     block_order,
@@ -409,22 +522,8 @@
     col_moment,
     next_tiles,
 ):
-    pre_float = pre_act.astype(jnp.float32)
-    activation = jax.nn.silu(pre_float).astype(jnp.bfloat16)
-    grad_act = lax.dot_general(
-        grad_output, pointwise_live, (((1,), (1,)), ((), ())), preferred_element_type=jnp.float32
-    )
-    grad_pre = (grad_act * silu_slope(pre_float)).astype(jnp.bfloat16)
-    pieces = [contract_rows(view, grad_pre) for view in tap_views(saved_tiles[0])]
-    pieces.append(contract_rows(activation, grad_output))
-    own_term = jnp.concatenate(pieces, axis=0).astype(jnp.bfloat16)
-    total_rows = NB * BLK
-    order = block_order.reshape(4, 4, 2, OWN).transpose(2, 1, 0, 3)
-    quarters = jnp.arange(4, dtype=jnp.int32)[None, None, :, None, None]
-    source = order[:, :, None] * 4 + quarters
-    tiles = own_term.reshape(NB, 2, 16, 2, 128).transpose(0, 1, 3, 2, 4).reshape(NB * 4, 16, 128)
-    term = jnp.take(tiles, source.reshape(-1), axis=0).reshape(2, 4, 4, 4, OWN, 16, 128)
-
+    term = backward(block_order, saved_tiles, pre_act, grad_output, pointwise_live)
+    term = term.reshape(2, 4, 4, 4, OWN, 16, 128)
     owner = lax.axis_index("shard")
     own_blocks = lax.dynamic_slice_in_dim(block_order, owner * OWN, OWN)
     is_small = (own_blocks >= NB3).astype(jnp.float32)
@@ -442,21 +541,8 @@
     update, new_master, new_row, new_col, gathered = optimizer_step(
         term, aux, row_moment.reshape(OWN, BLK, 1), master_rows.reshape(OWN, BLK, CO)
     )
-    position = jnp.zeros((NB,), jnp.int32).at[order.reshape(-1)].set(jnp.arange(NB, dtype=jnp.int32))
-    outer, inner = position // 28, position % 28
-    place = outer[:, None] * 112 + jnp.arange(4, dtype=jnp.int32)[None, :] * 28 + inner[:, None]
-    natural = jnp.take(gathered.reshape(NB * 4, 16, 128), place.reshape(-1), axis=0)
-    natural = natural.reshape(NB, 2, 2, 16, 128).transpose(0, 1, 3, 2, 4).reshape(total_rows, CO)
-    spatial = natural[: 27 * CI].reshape(27, CI, CO)
-    pointwise = natural[27 * CI :]
-    hidden_sum = jnp.zeros((FR * HW * HW, CO), jnp.float32)
-    for index_tap, view in enumerate(tap_views(next_tiles[0])):
-        hidden_sum = hidden_sum + jnp.dot(
-            view, spatial[index_tap], preferred_element_type=jnp.float32
-        )
-    hidden_act = jax.nn.silu(hidden_sum).astype(jnp.bfloat16)
-    next_output = jnp.dot(hidden_act, pointwise, preferred_element_type=jnp.float32).astype(
-        jnp.bfloat16
+    next_output, update, new_master = forward(
+        block_order, next_tiles, gathered.reshape(8, 4, 28, 16, 128), update, new_master
     )
     return (
         update.reshape(master_rows.shape),

time: 199 us -> 136 us (0.68)
  matrix products: 39.6 us -> 0 us
  local copies, waits for them, and re-layouts: 39.5 us -> 7.93 us
  Pallas kernels: 105 us -> 126 us
  other arithmetic: 12.2 us -> 0.86 us
    dot_general x56 -> x0, matrix products: 39.6 us -> none  [the longest x28 26.2 us: contract_rows(): lax.dot_general(left, right, (((0,), (0,)), ((), ())), preferred_element_...]
    pallas_call x0 -> x2, Pallas kernels: none -> 20.5 us  [the longest x1 11.1 us: backward(): pl.pallas_call(backward_kernel, name='backward', out_shape=jax.ShapeDtype...]
    convert_element_type x2 -> x0, local copies, waits for them, and re-layouts: 11.1 us -> none  [shards(): own_term = jnp.concatenate(pieces, axis=0).astype(jnp.bfloat16)]
    select_n x5 -> x0, other arithmetic: 11 us -> none  [the longest x2 6.09 us: shards(): jnp.take(tiles, source.reshape(-1), axis=0)]
    gather x2 -> x0, local copies, waits for them, and re-layouts: 10.7 us -> none  [the longest x1 5.33 us: shards(): jnp.take(tiles, source.reshape(-1), axis=0)]
    slice x34 -> x0, local copies, waits for them, and re-layouts: 7.13 us -> none  [the longest x29 3.95 us: shards(): spatial[index_tap]]
    unnamed x20 -> x8, local copies, waits for them, and re-layouts: 4.51 us -> 3.18 us
where the time goes in v2:
time: 136 us
  Pallas kernels  126 us (93%)
  local copies, waits for them, and re-layouts  7.93 us (6%)
  between operations  1.41 us (1%)
    pallas_call x1, Pallas kernels, optimizer_step(): pl.pallas_call(step_kernel, name='optimizer_step', out_shape=(jax.ShapeDt...  105 us
    pallas_call x1, Pallas kernels, backward(): pl.pallas_call(backward_kernel, name='backward', out_shape=jax.ShapeDtype...  11.1 us
    pallas_call x1, Pallas kernels, forward(): pl.pallas_call(forward_kernel, name='forward', out_shape=(jax.ShapeDtypeS...  9.34 us
    unnamed x8, local copies, waits for them, and re-layouts  3.18 us

profile of v2, /device:TPU:1, one launch (start us, length us, event | category | flops | bytes accessed | tf_op | source)
XLA Modules:
  0.0 135.9 jit_solution(9560689423130660715)
XLA Ops:
  0.6 0.0 copy-start.2
  0.6 0.8 compare_convert_fusion
  1.4 0.1 broadcast_in_dim.17
  2.2 1.9 %concatenate.3.aux = f32[16,256]{1,0:T(8,128)} concatenate(f32[1,256]{1,0:T(1,128)S(1)} %broadcast_in_dim.15, f32[2,256]{1,0:T(2,128)} %param.18, f32[5,256]{1,0:T(8,128)S(1)} %broadcast_in_dim.16, f32[7,256]{1,0:T(8,128)S(1)} %broadcast_in_dim.17, f32[1,256]{1,0:T(1,128)S(1)} %broadcast_in_dim.18), dimensions={0} | concatenate | bytes 32768 | tf_op jit(solution)/shard_map/concatenate | solution.py:531
  4.1 2.1 %copy.17.tiles = bf16[1,4,18,18,256]{4,3,2,1,0:T(8,128)(2,1)} copy(bf16[1,4,18,18,256]{4,1,3,2,0:T(4,128)(2,1)} %param.12) | data formatting | bytes 1327104 | tf_op args[2]
  6.2 0.0 copy-start
  6.2 11.1 %backward.1 = bf16[8,4,28,16,128]{4,3,2,1,0:T(8,128)(2,1)} custom-call(s32[224]{0:T(256)} %order.3, bf16[1,4,18,18,256]{4,3,2,1,0:T(8,128)(2,1)} %copy.17.tiles, bf16[512,256]{1,0:T(8,128)(2,1)} %pre.1, bf16[512,256]{1,0:T(8,128)(2,1)} %grad_out.1, bf16[256,256]{1,0:T(8,128)(2,1)} %live.1), custom_call_target="tpu_custom_call" | custom-call | tf_op jit(solution)/shard_map/backward/pallas_call | solution.py:441
  17.4 0.0 copy-done.2
  17.4 0.9 reshape.43.row_in
  18.2 105.3 %optimizer_step.1 = (f32[7,32,256]{2,1,0:T(8,128)}, f32[7,32,256]{2,1,0:T(8,128)}, f32[7,32,1]{2,1,0:T(8,128)}, f32[8,256]{1,0:T(8,128)}, bf16[2,4,4,4,7,16,128]{6,5,4,3,2,1,0:T(8,128)(2,1)}) custom-call(bf16[2,4,4,4,7,16,128]{6,5,4,3,2,1,0:T(8,128)(2,1)} %bitcast.6, f32[16,256]{1,0:T(8,128)} %concatenate.3.aux, f32[7,32,1]{2,1,0:T(8,128)} %reshape.43.row_in, ...), custom_call_target="tpu_custom_call" | custom-call | tf_op jit(solution)/shard_map/optimizer_step/pallas_call | solution.py:342
  123.5 0.0 copy-start.1
  123.5 0.0 copy-done
  123.5 1.0 copy.19.tiles
  124.5 9.3 %forward.1 = (bf16[512,256]{1,0:T(8,128)(2,1)}, f32[7,32,256]{2,1,0:T(8,128)}, f32[7,32,256]{2,1,0:T(8,128)}) custom-call(s32[224]{0:T(256)} %order.3, bf16[1,4,18,18,256]{4,3,2,1,0:T(8,128)(2,1)} %copy.19.tiles, bf16[8,4,28,16,128]{4,3,2,1,0:T(8,128)(2,1)} %bitcast.7, f32[7,32,256]{2,1,0:T(8,128)} %get-tuple-element.14.update_in, ...), custom_call_target="tpu_custom_call" | custom-call | tf_op jit(solution)/shard_map/forward/pallas_call | solution.py:495
  133.9 0.0 copy-done.1
  133.9 0.1 reduce
  134.0 0.6 reshape.42
  134.6 1.3 slice.3
  (3 shorter events, 0.0 us)
Async XLA Ops:
  0.6 16.7 %copy-start.2 = (f32[224]{0:T(256)S(1)}, f32[224]{0:T(256)}, u32[]{:S(2)}) copy-start(f32[224]{0:T(256)} %param.17) | copy-start | bytes 2692
  6.2 117.2 %copy-start = (bf16[1,4,18,18,256]{4,1,3,2,0:T(4,128)(2,1)S(1)}, bf16[1,4,18,18,256]{4,1,3,2,0:T(4,128)(2,1)}, u32[]{:S(2)}) copy-start(bf16[1,4,18,18,256]{4,1,3,2,0:T(4,128)(2,1)} %param.19) | copy-start | bytes 1990660
  123.5 10.4 %copy-start.1 = (f32[7,32,1]{2,1,0:T(8,128)S(1)}, f32[7,32,1]{2,1,0:T(8,128)}, u32[]{:S(2)}) copy-start(f32[7,32,1]{2,1,0:T(8,128)} %get-tuple-element.18) | copy-start | bytes 2692

commit v3 on v2

--- a/solution.py
+++ b/solution.py
@@ -33,12 +33,12 @@
     new_col,
     weights,
     core_in,
-    y_sum,
-    y_half,
-    y_full,
-    x_sum,
-    x_half,
-    x_full,
+    first_sum,
+    first_half,
+    first_full,
+    last_sum,
+    last_half,
+    last_full,
     z_sum,
     z_in,
     h_in,
@@ -110,85 +110,129 @@
                 total = total + read(step).astype(f32)
             dst(step, total.astype(bf16))
 
+    coords = ((y, x), (x, y))
+    devices = ((dev_y, dev_x), (dev_x, dev_y))
+
+    def cell(stream, i, j):
+        return (i, j) if stream == 0 else (j, i)
+
     core_copies = {}
+    pair = (pl.ds(0, 2), pl.ds(2, 2))
     for d in (2, 1, 3, 0):
         j = (y + d) % 4
-        core_copies[d] = send(term.at[1 - c, j], core_in.at[j], dev_core())
-
-    def y_part(d, start, count, more=()):
-        j = (y + d) % 4
-
-        def put(step, value):
-            y_sum[d, start + step // 4, step % 4] = value
-
-        reads = [
-            lambda step: term[c, j, start + step // 4, step % 4],
-            lambda step: core_in[j, start + step // 4, step % 4],
-        ]
-        for slot in more:
-            reads.append(lambda step, slot=slot: y_half[slot, step // 4, step % 4])
-        add_into(put, 4 * count, reads)
-
-    core_copies[2].wait_recv()
-    y_part(2, 0, 2)
-    half_0 = send(y_sum.at[2, pl.ds(0, 2)], y_half.at[0], dev_y(1))
-    y_part(2, 2, 2)
-    half_1 = send(y_sum.at[2, pl.ds(2, 2)], y_half.at[1], dev_y(3))
-    core_copies[1].wait_recv()
-    y_part(1, 2, 2)
-    full_0b = send(y_sum.at[1, pl.ds(2, 2)], y_full.at[0, pl.ds(2, 2)], dev_y(1))
-    core_copies[3].wait_recv()
-    y_part(3, 0, 2)
-    full_1a = send(y_sum.at[3, pl.ds(0, 2)], y_full.at[1, pl.ds(0, 2)], dev_y(3))
-    half_0.wait_recv()
-    y_part(1, 0, 2, more=(0,))
-    full_0a = send(y_sum.at[1, pl.ds(0, 2)], y_full.at[0, pl.ds(0, 2)], dev_y(1))
-    half_1.wait_recv()
-    y_part(3, 2, 2, more=(1,))
-    full_1b = send(y_sum.at[3, pl.ds(2, 2)], y_full.at[1, pl.ds(2, 2)], dev_y(3))
-    core_copies[0].wait_recv()
-    for copy in (full_0b, full_1a, full_0a, full_1b):
-        copy.wait_recv()
-
-    def x_part(d, start, count, more=()):
-        q = (x + d) % 4
-
-        def put(step, value):
-            x_sum[d, start + step] = value
-
-        reads = [
-            lambda step: term[c, y, q, start + step],
-            lambda step: core_in[y, q, start + step],
-            lambda step: y_full[0, q, start + step],
-            lambda step: y_full[1, q, start + step],
-        ]
-        for slot in more:
-            reads.append(lambda step, slot=slot: x_half[slot, step])
-        add_into(put, count, reads)
-
-    x_part(2, 0, 2)
-    half_0 = send(x_sum.at[2, pl.ds(0, 2)], x_half.at[0], dev_x(1))
-    x_part(2, 2, 2)
-    half_1 = send(x_sum.at[2, pl.ds(2, 2)], x_half.at[1], dev_x(3))
-    x_part(1, 2, 2)
-    full_0b = send(x_sum.at[1, pl.ds(2, 2)], x_full.at[0, pl.ds(2, 2)], dev_x(1))
-    x_part(3, 0, 2)
-    full_1a = send(x_sum.at[3, pl.ds(0, 2)], x_full.at[1, pl.ds(0, 2)], dev_x(3))
-    half_0.wait_recv()
-    x_part(1, 0, 2, more=(0,))
-    full_0a = send(x_sum.at[1, pl.ds(0, 2)], x_full.at[0, pl.ds(0, 2)], dev_x(1))
-    half_1.wait_recv()
-    x_part(3, 2, 2, more=(1,))
-    full_1b = send(x_sum.at[3, pl.ds(2, 2)], x_full.at[1, pl.ds(2, 2)], dev_x(3))
-    x_part(0, 0, 4)
-    for copy in (full_0b, full_1a, full_0a, full_1b):
-        copy.wait_recv()
+        core_copies[0, d] = send(
+            term.at[1 - c, j, :, pair[0]], core_in.at[j, :, pair[0]], dev_core()
+        )
+        j = (x + d) % 4
+        core_copies[1, d] = send(
+            term.at[1 - c, :, j, pair[1]], core_in.at[:, j, pair[1]], dev_core()
+        )
+
+    def reduce_stream(stream):
+        first, last = coords[stream]
+        dev_first, dev_last = devices[stream]
+        base = 2 * stream
+
+        def first_part(d, start, more=()):
+            i = (first + d) % 4
+
+            def put(step, value):
+                first_sum[stream, d, start + step // 2, step % 2] = value
+
+            def here(step):
+                return cell(stream, i, start + step // 2) + (base + step % 2,)
+
+            reads = [
+                lambda step: term[(c,) + here(step)],
+                lambda step: core_in[here(step)],
+            ]
+            for slot in more:
+                reads.append(lambda step, slot=slot: first_half[stream, slot, step // 2, step % 2])
+            add_into(put, 4, reads)
+
+        def pass_on(d, start, slot, step):
+            span = pl.ds(start, 2)
+            return send(
+                first_sum.at[stream, d, span], first_full.at[stream, slot, span], dev_first(step)
+            )
+
+        core_copies[stream, 2].wait_recv()
+        first_part(2, 0)
+        half_0 = send(first_sum.at[stream, 2, pair[0]], first_half.at[stream, 0], dev_first(1))
+        first_part(2, 2)
+        half_1 = send(first_sum.at[stream, 2, pair[1]], first_half.at[stream, 1], dev_first(3))
+        yield
+        core_copies[stream, 1].wait_recv()
+        first_part(1, 2)
+        fulls = [pass_on(1, 2, 0, 1)]
+        core_copies[stream, 3].wait_recv()
+        first_part(3, 0)
+        fulls.append(pass_on(3, 0, 1, 3))
+        yield
+        half_0.wait_recv()
+        first_part(1, 0, more=(0,))
+        fulls.append(pass_on(1, 0, 0, 1))
+        half_1.wait_recv()
+        first_part(3, 2, more=(1,))
+        fulls.append(pass_on(3, 2, 1, 3))
+        core_copies[stream, 0].wait_recv()
+        yield
+        for copy in fulls:
+            copy.wait_recv()
+
+        def last_part(d, start, count, more=()):
+            q = (last + d) % 4
+            place = cell(stream, first, q)
+
+            def put(step, value):
+                last_sum[stream, d, start + step] = value
+
+            reads = [
+                lambda step: term[(c,) + place + (base + start + step,)],
+                lambda step: core_in[place + (base + start + step,)],
+                lambda step: first_full[stream, 0, q, start + step],
+                lambda step: first_full[stream, 1, q, start + step],
+            ]
+            for slot in more:
+                reads.append(lambda step, slot=slot: last_half[stream, slot])
+            add_into(put, count, reads)
+
+        def pass_last(d, start, slot, step):
+            return send(
+                last_sum.at[stream, d, start], last_full.at[stream, slot, start], dev_last(step)
+            )
+
+        last_part(2, 0, 1)
+        half_0 = send(last_sum.at[stream, 2, 0], last_half.at[stream, 0], dev_last(1))
+        last_part(2, 1, 1)
+        half_1 = send(last_sum.at[stream, 2, 1], last_half.at[stream, 1], dev_last(3))
+        last_part(1, 1, 1)
+        fulls = [pass_last(1, 1, 0, 1)]
+        last_part(3, 0, 1)
+        fulls.append(pass_last(3, 0, 1, 3))
+        last_part(0, 0, 2)
+        yield
+        half_0.wait_recv()
+        last_part(1, 0, 1, more=(0,))
+        fulls.append(pass_last(1, 0, 0, 1))
+        half_1.wait_recv()
+        last_part(3, 1, 1, more=(1,))
+        fulls.append(pass_last(3, 1, 1, 3))
+        yield
+        for copy in fulls:
+            copy.wait_recv()
+        yield
+
+    for _ in zip(reduce_stream(0), reduce_stream(1)):
+        pass
 
     z_copies = []
     for d in (3, 2, 1, 0):
         z = (zl + d) % 4
         z_sum[d] = (
-            x_sum[0, z].astype(f32) + x_full[0, z].astype(f32) + x_full[1, z].astype(f32)
+            last_sum[z // 2, 0, z % 2].astype(f32)
+            + last_full[z // 2, 0, z % 2].astype(f32)
+            + last_full[z // 2, 1, z % 2].astype(f32)
         ).astype(bf16)
         if d:
             z_copies.append(send(z_sum.at[d], z_in.at[d - 1], dev_z(d)))
@@ -299,31 +343,53 @@
     ]
     for copy in z_copies:
         copy.wait_recv()
-    to_right = send(weights.at[c, y, x], weights.at[c, y, x], dev_x(1))
-    to_left = send(weights.at[c, y, x], weights.at[c, y, x], dev_x(3))
-    to_right.wait_recv()
-    low, high = pl.ds(0, 2), pl.ds(2, 2)
-    on_right = send(weights.at[c, y, left, low], weights.at[c, y, left, low], dev_x(1))
-    to_left.wait_recv()
-    on_left = send(weights.at[c, y, right, high], weights.at[c, y, right, high], dev_x(3))
-    on_right.wait_recv()
-    on_left.wait_recv()
-    below = (y + 3) % 4
-    above = (y + 1) % 4
-    across = (y + 2) % 4
-    to_above = send(weights.at[c, y], weights.at[c, y], dev_y(1))
-    to_below = send(weights.at[c, y], weights.at[c, y], dev_y(3))
-    cores = [send(weights.at[c, y], weights.at[c, y], dev_core())]
-    to_above.wait_recv()
-    on_above = send(weights.at[c, below, low], weights.at[c, below, low], dev_y(1))
-    cores.append(send(weights.at[c, below], weights.at[c, below], dev_core()))
-    to_below.wait_recv()
-    on_below = send(weights.at[c, above, high], weights.at[c, above, high], dev_y(3))
-    cores.append(send(weights.at[c, above], weights.at[c, above], dev_core()))
-    on_above.wait_recv()
-    cores.append(send(weights.at[c, across, low], weights.at[c, across, low], dev_core()))
-    on_below.wait_recv()
-    cores.append(send(weights.at[c, across, high], weights.at[c, across, high], dev_core()))
+    cores = []
+
+    def gather_stream(stream):
+        first, last = coords[stream]
+        dev_first, dev_last = devices[stream]
+        base = 2 * stream
+        both = pl.ds(base, 2)
+
+        def spread(place, device):
+            return send(weights.at[place], weights.at[place], device)
+
+        def at_last(q, z):
+            return (c,) + cell(stream, first, q) + (z,)
+
+        def at_first(i, j):
+            return (c,) + cell(stream, i, j) + (both,)
+
+        up = spread(at_last(last, both), dev_last(1))
+        down = spread(at_last(last, both), dev_last(3))
+        up.wait_recv()
+        on_up = spread(at_last((last + 3) % 4, base), dev_last(1))
+        down.wait_recv()
+        on_down = spread(at_last((last + 1) % 4, base + 1), dev_last(3))
+        yield
+        on_up.wait_recv()
+        on_down.wait_recv()
+        whole = slice(None)
+        up = spread(at_first(first, whole), dev_first(1))
+        down = spread(at_first(first, whole), dev_first(3))
+        cores.append(spread(at_first(first, whole), dev_core()))
+        yield
+        before, after, across = (first + 3) % 4, (first + 1) % 4, (first + 2) % 4
+        up.wait_recv()
+        on_up = spread(at_first(before, pair[0]), dev_first(1))
+        cores.append(spread(at_first(before, whole), dev_core()))
+        down.wait_recv()
+        on_down = spread(at_first(after, pair[1]), dev_first(3))
+        cores.append(spread(at_first(after, whole), dev_core()))
+        yield
+        on_up.wait_recv()
+        cores.append(spread(at_first(across, pair[0]), dev_core()))
+        on_down.wait_recv()
+        cores.append(spread(at_first(across, pair[1]), dev_core()))
+        yield
+
+    for _ in zip(gather_stream(0), gather_stream(1)):
+        pass
     for copy in cores:
         copy.wait_recv()
     assert len(started) == N_COPIES
@@ -331,7 +397,7 @@
         copy.wait_send()
 
 
-N_COPIES = 49
+N_COPIES = 78
 
 
 def optimizer_step(term, aux, row_in, master):
@@ -353,12 +419,12 @@
         out_specs=[vmem] * 5,
         scratch_shapes=[
             pltpu.VMEM((4, 4, 4) + tile, bf16),
-            pltpu.VMEM((4, 4, 4) + tile, bf16),
-            pltpu.VMEM((2, 2, 4) + tile, bf16),
-            pltpu.VMEM((2, 4, 4) + tile, bf16),
-            pltpu.VMEM((4, 4) + tile, bf16),
+            pltpu.VMEM((2, 4, 4, 2) + tile, bf16),
+            pltpu.VMEM((2, 2, 2, 2) + tile, bf16),
+            pltpu.VMEM((2, 2, 4, 2) + tile, bf16),
+            pltpu.VMEM((2, 4, 2) + tile, bf16),
             pltpu.VMEM((2, 2) + tile, bf16),
-            pltpu.VMEM((2, 4) + tile, bf16),
+            pltpu.VMEM((2, 2, 2) + tile, bf16),
             pltpu.VMEM((4,) + tile, bf16),
             pltpu.VMEM((3,) + tile, bf16),
             pltpu.VMEM((4,) + tile, bf16),
@@ -391,8 +457,43 @@
             visit(order[owner * OWN + i], outer, (owner // 8) * OWN + i)
 
 
-def backward_kernel(order, tiles, pre, grad_out, live, term, shifted, left, right, act, outer, inner):
+def diagonal(shape):
+    return lax.broadcasted_iota(jnp.int32, shape, 0) == lax.broadcasted_iota(jnp.int32, shape, 1)
+
+
+def backward_kernel(
+    order,
+    step_count,
+    tiles,
+    pre,
+    grad_out,
+    live,
+    col_moment,
+    row_moment,
+    term,
+    aux,
+    row_column,
+    shifted,
+    left,
+    right,
+    act,
+    outer,
+    inner,
+):
     f32 = jnp.float32
+    owner = lax.axis_index("shard")
+    steps = jnp.full((1, CO), step_count[0], jnp.int32).astype(f32)
+    aux[0:1, :] = 1.0 - jnp.exp(-decay_power * jnp.log(steps))
+    aux[1:3, :] = col_moment[...]
+    aux[3:8, :] = jnp.zeros((5, CO), f32)
+    for i in range(OWN):
+        flag = jnp.where(order[owner * OWN + i] >= NB3, 1.0, 0.0).astype(f32)
+        aux[8 + i : 9 + i, :] = jnp.full((1, CO), flag, f32)
+    aux[15:16, :] = jnp.zeros((1, CO), f32)
+    rows = OWN * BLK
+    row_column[...] = jnp.sum(
+        jnp.where(diagonal((rows, rows)), row_moment[...], 0.0), axis=1, keepdims=True
+    )
     bf16 = jnp.bfloat16
 
     def note(block, outer_place, inner_place):
@@ -434,16 +535,29 @@
     emit(NB3, jnp.dot(right[...], act[...], preferred_element_type=f32))
 
 
-def backward(block_order, saved_tiles, pre_act, grad_output, pointwise_live):
+def backward(
+    block_order,
+    step_count,
+    saved_tiles,
+    pre_act,
+    grad_output,
+    pointwise_live,
+    col_moment,
+    row_moment,
+):
     bf16 = jnp.bfloat16
     vmem = pl.BlockSpec(memory_space=pltpu.VMEM)
     smem = pl.BlockSpec(memory_space=pltpu.SMEM)
     return pl.pallas_call(
         backward_kernel,
         name="backward",
-        out_shape=jax.ShapeDtypeStruct((8, 4, 28, 16, 128), bf16),
-        in_specs=[smem] + [vmem] * 4,
-        out_specs=vmem,
+        out_shape=(
+            jax.ShapeDtypeStruct((8, 4, 28, 16, 128), bf16),
+            jax.ShapeDtypeStruct((16, CO), jnp.float32),
+            jax.ShapeDtypeStruct((OWN * BLK, 1), jnp.float32),
+        ),
+        in_specs=[smem] * 2 + [vmem] * 6,
+        out_specs=[vmem] * 3,
         scratch_shapes=[
             pltpu.VMEM((3, FR + 2, HW + 2, HW, CI), bf16),
             pltpu.VMEM((CO, FR * HW * HW), bf16),
@@ -452,13 +566,41 @@
             pltpu.SMEM((NB,), jnp.int32),
             pltpu.SMEM((NB,), jnp.int32),
         ],
-    )(block_order, saved_tiles, pre_act, grad_output, pointwise_live)
+    )(
+        block_order,
+        step_count,
+        saved_tiles,
+        pre_act,
+        grad_output,
+        pointwise_live,
+        col_moment,
+        row_moment.reshape(1, OWN * BLK),
+    )
 
 
 def forward_kernel(
-    order, tiles, gathered, update_in, master_in, output, update, master, shifted, kernels, hidden
+    order,
+    tiles,
+    gathered,
+    update_in,
+    master_in,
+    row_in,
+    col_in,
+    output,
+    update,
+    master,
+    new_row,
+    new_col,
+    shifted,
+    kernels,
+    hidden,
 ):
     f32 = jnp.float32
+    rows = OWN * BLK
+    new_row[...] = jnp.sum(
+        jnp.where(diagonal((rows, rows)), row_in[...], 0.0), axis=0, keepdims=True
+    )
+    new_col[...] = col_in[0:2, :]
     update[...] = update_in[...]
     master[...] = master_in[...]
     shift_columns(tiles, shifted)
@@ -487,7 +629,7 @@
         output[rows, :] = jnp.dot(acted, pointwise, preferred_element_type=f32).astype(jnp.bfloat16)
 
 
-def forward(block_order, next_tiles, gathered, update, master):
+def forward(block_order, next_tiles, gathered, update, master, row, col):
     bf16 = jnp.bfloat16
     f32 = jnp.float32
     vmem = pl.BlockSpec(memory_space=pltpu.VMEM)
@@ -499,15 +641,17 @@
             jax.ShapeDtypeStruct((FR * HW * HW, CO), bf16),
             jax.ShapeDtypeStruct(update.shape, f32),
             jax.ShapeDtypeStruct(master.shape, f32),
+            jax.ShapeDtypeStruct((1, OWN * BLK), f32),
+            jax.ShapeDtypeStruct((2, CO), f32),
         ),
-        in_specs=[smem] + [vmem] * 4,
-        out_specs=[vmem] * 3,
+        in_specs=[smem] + [vmem] * 6,
+        out_specs=[vmem] * 5,
         scratch_shapes=[
             pltpu.VMEM((3, FR + 2, HW + 2, HW, CI), bf16),
             pltpu.VMEM((NB, 2, 16, CO), bf16),
             pltpu.VMEM((FR * HW * HW, CO), f32),
         ],
-    )(block_order, next_tiles, gathered, update, master)
+    )(block_order, next_tiles, gathered, update, master, row, col)
 
 
 def shards(
@@ -522,33 +666,34 @@
     col_moment,
     next_tiles,
 ):
-    term = backward(block_order, saved_tiles, pre_act, grad_output, pointwise_live)
+    term, aux, row_column = backward(
+        block_order,
+        step_count,
+        saved_tiles,
+        pre_act,
+        grad_output,
+        pointwise_live,
+        col_moment,
+        row_moment,
+    )
     term = term.reshape(2, 4, 4, 4, OWN, 16, 128)
-    owner = lax.axis_index("shard")
-    own_blocks = lax.dynamic_slice_in_dim(block_order, owner * OWN, OWN)
-    is_small = (own_blocks >= NB3).astype(jnp.float32)
-    decay_rate = 1.0 - step_count.astype(jnp.float32)[0] ** (-decay_power)
-    aux = jnp.concatenate(
-        [
-            jnp.broadcast_to(decay_rate, (1, CO)),
-            col_moment,
-            jnp.zeros((5, CO), jnp.float32),
-            jnp.broadcast_to(is_small[:, None], (OWN, CO)),
-            jnp.zeros((1, CO), jnp.float32),
-        ],
-        axis=0,
+    update, new_master, new_row, new_col, gathered = optimizer_step(
+        term, aux, row_column.reshape(OWN, BLK, 1), master_rows.reshape(OWN, BLK, CO)
     )
-    update, new_master, new_row, new_col, gathered = optimizer_step(
-        term, aux, row_moment.reshape(OWN, BLK, 1), master_rows.reshape(OWN, BLK, CO)
-    )
-    next_output, update, new_master = forward(
-        block_order, next_tiles, gathered.reshape(8, 4, 28, 16, 128), update, new_master
+    next_output, update, new_master, new_row, new_col = forward(
+        block_order,
+        next_tiles,
+        gathered.reshape(8, 4, 28, 16, 128),
+        update,
+        new_master,
+        new_row.reshape(OWN * BLK, 1),
+        new_col,
     )
     return (
         update.reshape(master_rows.shape),
         new_master.reshape(master_rows.shape),
         new_row.reshape(row_moment.shape),
-        new_col[:2],
+        new_col,
         next_output,
     )
 

time: 136 us -> 120 us (0.88)
  Pallas kernels: 126 us -> 116 us
  local copies, waits for them, and re-layouts: 7.93 us -> 3.23 us
    pallas_call x1, Pallas kernels: 105 us -> 95.1 us  [optimizer_step(): pl.pallas_call(step_kernel, name='optimizer_step', out_shape=(jax.ShapeDt...]
    concatenate x1 -> x0, local copies, waits for them, and re-layouts: 1.9 us -> none  [shards(): jnp.concatenate([jnp.broadcast_to(decay_rate, (1, CO)), col_moment, jnp.z...]
    reshape x2 -> x0, local copies, waits for them, and re-layouts: 1.5 us -> none  [the longest x1 0.85 us: shards(): row_moment.reshape(OWN, BLK, 1)]
    unnamed x8 -> x4, local copies, waits for them, and re-layouts: 3.18 us -> 3.23 us
where the time goes in v3:
time: 120 us
  Pallas kernels  116 us (97%)
  local copies, waits for them, and re-layouts  3.23 us (3%)
  between operations  1.31 us (1%)
    pallas_call x1, Pallas kernels, optimizer_step(): pl.pallas_call(step_kernel, name='optimizer_step', out_shape=(jax.ShapeDt...  95.1 us
    pallas_call x1, Pallas kernels, backward(): pl.pallas_call(backward_kernel, name='backward', out_shape=(jax.ShapeDtyp...  11.2 us
    pallas_call x1, Pallas kernels, forward(): pl.pallas_call(forward_kernel, name='forward', out_shape=(jax.ShapeDtypeS...  9.44 us
    unnamed x4, local copies, waits for them, and re-layouts  3.23 us

profile of v3, /device:TPU:1, one launch (start us, length us, event | category | flops | bytes accessed | tf_op | source)
XLA Modules:
  0.0 120.2 jit_solution(9325945998267869668)
XLA Ops:
  0.6 0.0 copy-start
  0.6 2.2 %copy.15.tiles = bf16[1,4,18,18,256]{4,3,2,1,0:T(8,128)(2,1)} copy(bf16[1,4,18,18,256]{4,1,3,2,0:T(4,128)(2,1)} %param.12) | data formatting | bytes 1327104 | tf_op args[2]
  3.5 11.2 %backward.1 = (bf16[8,4,28,16,128]{4,3,2,1,0:T(8,128)(2,1)}, f32[16,256]{1,0:T(8,128)}, f32[224,1]{1,0:T(8,128)}) custom-call(s32[224]{0:T(256)} %order.3, s32[1]{0:T(128)S(6)} %copy.17.step_count, bf16[1,4,18,18,256]{4,3,2,1,0:T(8,128)(2,1)} %copy.15.tiles, bf16[512,256]{1,0:T(8,128)(2,1)} %pre.1, bf16[512,256]{1,0:T(8,128)(2,1)} %grad_out.1, ...), custom_call_target="tpu_custom_call" | custom-call | tf_op jit(solution)/shard_map/backward/pallas_call | solution.py:551
  14.7 95.1 %optimizer_step.1 = (f32[7,32,256]{2,1,0:T(8,128)}, f32[7,32,256]{2,1,0:T(8,128)}, f32[7,32,1]{2,1,0:T(8,128)}, f32[8,256]{1,0:T(8,128)}, bf16[2,4,4,4,7,16,128]{6,5,4,3,2,1,0:T(8,128)(2,1)}) custom-call(bf16[2,4,4,4,7,16,128]{6,5,4,3,2,1,0:T(8,128)(2,1)} %bitcast.10, f32[16,256]{1,0:T(8,128)} %get-tuple-element.19.aux, f32[7,32,1]{2,1,0:T(8,128)} %bitcast.13, ...), custom_call_target="tpu_custom_call" | custom-call | tf_op jit(solution)/shard_map/optimizer_step/pallas_call | solution.py:408
  109.7 0.0 copy-done
  109.7 1.0 copy.16.tiles
  110.8 9.4 %forward.1 = (bf16[512,256]{1,0:T(8,128)(2,1)}, f32[7,32,256]{2,1,0:T(8,128)}, f32[7,32,256]{2,1,0:T(8,128)}, f32[1,224]{1,0:T(1,128)}, f32[2,256]{1,0:T(2,128)}) custom-call(s32[224]{0:T(256)} %order.3, bf16[1,4,18,18,256]{4,3,2,1,0:T(8,128)(2,1)} %copy.16.tiles, bf16[8,4,28,16,128]{4,3,2,1,0:T(8,128)(2,1)} %bitcast.9, ...), custom_call_target="tpu_custom_call" | custom-call | tf_op jit(solution)/shard_map/forward/pallas_call | solution.py:637
Async XLA Ops:
  0.6 109.1 %copy-start = (bf16[1,4,18,18,256]{4,1,3,2,0:T(4,128)(2,1)S(1)}, bf16[1,4,18,18,256]{4,1,3,2,0:T(4,128)(2,1)}, u32[]{:S(2)}) copy-start(bf16[1,4,18,18,256]{4,1,3,2,0:T(4,128)(2,1)} %param.19) | copy-start | bytes 1990660

commit v4 on v3

--- a/solution.py
+++ b/solution.py
@@ -398,6 +398,7 @@
 
 
 N_COPIES = 78
+VMEM_GRANT = 28 * 1024 * 1024
 
 
 def optimizer_step(term, aux, row_in, master):
@@ -436,12 +437,14 @@
             pltpu.SemaphoreType.DMA((N_COPIES,)),
             pltpu.SemaphoreType.DMA((N_COPIES,)),
         ],
-        compiler_params=pltpu.CompilerParams(collective_id=0, has_side_effects=True),
+        compiler_params=pltpu.CompilerParams(
+            collective_id=0, has_side_effects=True, vmem_limit_bytes=VMEM_GRANT
+        ),
     )(term, aux, row_in, master)
 
 
 def shift_columns(tiles, shifted):
-    @pl.loop(0, (FR + 2) * (HW + 2))
+    @pl.loop(0, (FR + 2) * (HW + 2), unroll=9)
     def _(step):
         frame, line = step // (HW + 2), step % (HW + 2)
         cells = tiles[0, frame, line].astype(jnp.float32)
@@ -450,7 +453,7 @@
 
 
 def each_stored_block(order, visit):
-    @pl.loop(0, 32)
+    @pl.loop(0, 32, unroll=4)
     def _(owner):
         outer = (owner % 2) * 4 + (owner // 2) % 4
         for i in range(OWN):
@@ -524,7 +527,7 @@
                 lane = 128 * (q % 2)
                 term[outer[block], q, inner[block]] = result[row : row + 16, lane : lane + 128]
 
-    @pl.loop(0, 9)
+    @pl.loop(0, 9, unroll=3)
     def _(spot):
         down, across = spot // 3, spot % 3
         for frame in range(3):
@@ -566,6 +569,7 @@
             pltpu.SMEM((NB,), jnp.int32),
             pltpu.SMEM((NB,), jnp.int32),
         ],
+        compiler_params=pltpu.CompilerParams(vmem_limit_bytes=VMEM_GRANT),
     )(
         block_order,
         step_count,
@@ -613,7 +617,7 @@
     each_stored_block(order, place)
     hidden[...] = jnp.zeros_like(hidden)
 
-    @pl.loop(0, 9)
+    @pl.loop(0, 9, unroll=3)
     def _(spot):
         down, across = spot // 3, spot % 3
         for frame in range(3):
@@ -651,6 +655,7 @@
             pltpu.VMEM((NB, 2, 16, CO), bf16),
             pltpu.VMEM((FR * HW * HW, CO), f32),
         ],
+        compiler_params=pltpu.CompilerParams(vmem_limit_bytes=VMEM_GRANT),
     )(block_order, next_tiles, gathered, update, master, row, col)
 
 

time: 120 us -> 112 us (0.933)
  Pallas kernels: 116 us -> 103 us
  local copies, waits for them, and re-layouts: 3.23 us -> 7.19 us
    pallas_call x1, Pallas kernels: 11.2 us -> 6.29 us  [backward(): pl.pallas_call(backward_kernel, name='backward', out_shape=(jax.ShapeDtyp...]
    unnamed x4 -> x18, local copies, waits for them, and re-layouts: 3.23 us -> 7.19 us
    pallas_call x1, Pallas kernels: 95.1 us -> 91.1 us  [optimizer_step(): pl.pallas_call(step_kernel, name='optimizer_step', out_shape=(jax.ShapeDt...]
    pallas_call x1, Pallas kernels: 9.44 us -> 5.8 us  [forward(): pl.pallas_call(forward_kernel, name='forward', out_shape=(jax.ShapeDtypeS...]
where the time goes in v4:
time: 112 us
  Pallas kernels  103 us (92%)
  local copies, waits for them, and re-layouts  7.19 us (6%)
  between operations  1.34 us (1%)
    pallas_call x1, Pallas kernels, optimizer_step(): pl.pallas_call(step_kernel, name='optimizer_step', out_shape=(jax.ShapeDt...  91.1 us
    unnamed x18, local copies, waits for them, and re-layouts  7.19 us
    pallas_call x1, Pallas kernels, backward(): pl.pallas_call(backward_kernel, name='backward', out_shape=(jax.ShapeDtyp...  6.29 us
    pallas_call x1, Pallas kernels, forward(): pl.pallas_call(forward_kernel, name='forward', out_shape=(jax.ShapeDtypeS...  5.8 us

profile of v4, /device:TPU:1, one launch (start us, length us, event | category | flops | bytes accessed | tf_op | source)
XLA Modules:
  0.0 111.7 jit_solution(8163926640755384)
XLA Ops:
  0.6 0.0 copy-start.7
  0.6 1.3 %copy.15.tiles = bf16[1,4,18,18,256]{4,3,2,1,0:T(8,128)(2,1)S(1)} copy(bf16[1,4,18,18,256]{4,1,3,2,0:T(4,128)(2,1)} %param.12) | data formatting | bytes 1327104 | tf_op args[2]
  2.6 0.0 copy-start
  2.6 0.9 copy-done
  3.5 0.0 copy-start.1
  3.5 0.9 copy-done.1
  4.5 0.0 copy-start.3
  4.5 0.9 copy-done.3
  5.4 0.0 copy-start.4
  5.4 0.7 copy-done.4
  6.1 0.0 copy-start.5
  6.1 0.7 copy-done.5
  6.7 0.0 copy-start.6
  6.8 0.7 copy-done.6
  7.4 6.3 %backward.1 = (bf16[8,4,28,16,128]{4,3,2,1,0:T(8,128)(2,1)S(1)}, f32[16,256]{1,0:T(8,128)S(1)}, f32[224,1]{1,0:T(8,128)S(1)}) custom-call(s32[224]{0:T(256)S(1)} %copy-done.4, s32[1]{0:T(128)S(6)} %copy.17.step_count, bf16[1,4,18,18,256]{4,3,2,1,0:T(8,128)(2,1)S(1)} %copy.15.tiles, bf16[512,256]{1,0:T(8,128)(2,1)S(1)} %copy-done, ...), custom_call_target="tpu_custom_call" | custom-call | tf_op jit(solution)/shard_map/backward/pallas_call | solution.py:554
  13.7 0.0 copy-start.2
  13.7 0.9 copy-done.2
  14.7 91.1 %optimizer_step.1 = (f32[7,32,256]{2,1,0:T(8,128)S(1)}, f32[7,32,256]{2,1,0:T(8,128)S(1)}, f32[7,32,1]{2,1,0:T(8,128)S(1)}, f32[8,256]{1,0:T(8,128)S(1)}, bf16[2,4,4,4,7,16,128]{6,5,4,3,2,1,0:T(8,128)(2,1)S(1)}) custom-call(bf16[2,4,4,4,7,16,128]{6,5,4,3,2,1,0:T(8,128)(2,1)S(1)} %bitcast.10, f32[16,256]{1,0:T(8,128)S(1)} %get-tuple-element.19.aux, ...), custom_call_target="tpu_custom_call" | custom-call | tf_op jit(solution)/shard_map/optimizer_step/pallas_call | solution.py:409
  105.8 0.0 copy-done.7
  105.8 0.1 copy.16.tiles
  105.9 5.8 %forward.1 = (bf16[512,256]{1,0:T(8,128)(2,1)}, f32[7,32,256]{2,1,0:T(8,128)}, f32[7,32,256]{2,1,0:T(8,128)}, f32[1,224]{1,0:T(1,128)}, f32[2,256]{1,0:T(2,128)}) custom-call(s32[224]{0:T(256)S(1)} %copy-done.4, bf16[1,4,18,18,256]{4,3,2,1,0:T(8,128)(2,1)S(1)} %copy.16.tiles, bf16[8,4,28,16,128]{4,3,2,1,0:T(8,128)(2,1)S(1)} %bitcast.9, ...), custom_call_target="tpu_custom_call" | custom-call | tf_op jit(solution)/shard_map/forward/pallas_call | solution.py:641
Async XLA Ops:
  0.6 105.2 %copy-start.7 = (bf16[1,4,18,18,256]{4,1,3,2,0:T(4,128)(2,1)S(1)}, bf16[1,4,18,18,256]{4,1,3,2,0:T(4,128)(2,1)}, u32[]{:S(2)}) copy-start(bf16[1,4,18,18,256]{4,1,3,2,0:T(4,128)(2,1)} %param.19) | copy-start | bytes 1990660
  2.6 1.0 copy-start
  3.5 0.9 copy-start.1
  4.5 0.9 copy-start.3
  5.4 0.7 copy-start.4
  6.1 0.7 copy-start.5
  6.7 0.7 copy-start.6
  13.7 0.9 copy-start.2

commit v5 on v4

--- a/solution.py
+++ b/solution.py
@@ -44,11 +44,11 @@
     h_in,
     grad,
     stat_own,
-    stat_core,
-    stat_y,
+    stat_plane,
     stat_z,
     send_sem,
     recv_sem,
+    relay,
 ):
     group = lax.axis_index("group")
     shard = lax.axis_index("shard")
@@ -70,6 +70,14 @@
     def dev_x(d):
         return (((x + d) % 4) * 4 + zh, shard)
 
+    def dev_plane(d, swap):
+        core = c + swap * (1 - 2 * c)
+        return (group, zl * 8 + ((y + d) % 4) * 2 + core)
+
+    def dev_line(d):
+        along = (zh * 4 + zl + d) % 16
+        return (x * 4 + along // 4, (along % 4) * 8 + y * 2 + c)
+
     def dev_h(d):
         return (x * 4 + (zh + d) % 4, shard)
 
@@ -77,11 +85,31 @@
     partners += [dev_y(d) for d in (1, 2, 3)]
     partners += [dev_x(d) for d in (1, 3)]
     partners += [dev_z(d) for d in (1, 2, 3)]
-    partners += [dev_h(d) for d in (1, 2, 3)]
+    partners += [dev_line(d) for d in (1, 15)]
+    partners += [dev_plane(d, 1) for d in (1, 2, 3)]
     barrier = pltpu.get_barrier_semaphore()
     for partner in partners:
         pl.semaphore_signal(barrier, inc=1, device_id=partner, device_id_type=MESH)
     pl.semaphore_wait(barrier, len(partners))
+
+    def tell(slot, device):
+        pl.semaphore_signal(relay.at[slot], inc=1, device_id=device, device_id_type=MESH)
+
+    tell(0, dev_line(1))
+    tell(1, dev_line(15))
+
+    def relay_step(level):
+        if level == 0:
+            pl.semaphore_wait(relay.at[0], 1)
+            pl.semaphore_wait(relay.at[1], 1)
+            tell(2, dev_line(2))
+            tell(3, dev_line(14))
+        elif level == 2:
+            pl.semaphore_wait(relay.at[2], 1)
+            pl.semaphore_wait(relay.at[3], 1)
+            tell(4, dev_line(4))
+        elif level == 4:
+            pl.semaphore_wait(relay.at[4], 1)
 
     started = []
 
@@ -223,8 +251,8 @@
             copy.wait_recv()
         yield
 
-    for _ in zip(reduce_stream(0), reduce_stream(1)):
-        pass
+    for level, _ in enumerate(zip(reduce_stream(0), reduce_stream(1))):
+        relay_step(level)
 
     z_copies = []
     for d in (3, 2, 1, 0):
@@ -298,12 +326,18 @@
             stat_own[4 + k : 5 + k, lanes] = jnp.broadcast_to(rows[k], (1, 128))
         stat_own[6:8, lanes] = jnp.zeros((2, 128), f32)
 
-    send(stat_own, stat_core, dev_core()).wait_recv()
-    stat_y[y] = stat_own[...] + stat_core[...]
-    y_copies = [send(stat_y.at[y], stat_y.at[y], dev_y(d)) for d in (2, 1, 3)]
-    for copy in y_copies:
+    stat_plane[c, y] = stat_own[...]
+    plane_copies = [
+        send(stat_plane.at[c, y], stat_plane.at[c, y], dev_plane(d, swap))
+        for d, swap in ((2, 1), (2, 0), (1, 1), (3, 1), (1, 0), (3, 0), (0, 1))
+    ]
+    for copy in plane_copies:
         copy.wait_recv()
-    stat_z[zl] = (stat_y[0] + stat_y[1]) + (stat_y[2] + stat_y[3])
+    by_core = [
+        (stat_plane[k, 0] + stat_plane[k, 1]) + (stat_plane[k, 2] + stat_plane[k, 3])
+        for k in range(2)
+    ]
+    stat_z[zl] = by_core[0] + by_core[1]
     z_copies = [send(stat_z.at[zl], stat_z.at[zl], dev_z(d)) for d in (3, 2, 1)]
     for copy in z_copies:
         copy.wait_recv()
@@ -397,7 +431,7 @@
         copy.wait_send()
 
 
-N_COPIES = 78
+N_COPIES = 81
 VMEM_GRANT = 28 * 1024 * 1024
 
 
@@ -431,11 +465,11 @@
             pltpu.VMEM((4,) + tile, bf16),
             pltpu.VMEM((4,) + tile, bf16),
             pltpu.VMEM((8, 256), f32),
-            pltpu.VMEM((8, 256), f32),
-            pltpu.VMEM((4, 8, 256), f32),
+            pltpu.VMEM((2, 4, 8, 256), f32),
             pltpu.VMEM((4, 8, 256), f32),
             pltpu.SemaphoreType.DMA((N_COPIES,)),
             pltpu.SemaphoreType.DMA((N_COPIES,)),
+            pltpu.SemaphoreType.REGULAR((5,)),
         ],
         compiler_params=pltpu.CompilerParams(
             collective_id=0, has_side_effects=True, vmem_limit_bytes=VMEM_GRANT

time: 112 us -> 109 us (0.973)
  Pallas kernels: 103 us -> 100 us
    pallas_call x1, Pallas kernels: 91.1 us -> 88.3 us  [optimizer_step(): pl.pallas_call(step_kernel, name='optimizer_step', out_shape=(jax.ShapeDt...]
where the time goes in v5:
time: 109 us
  Pallas kernels  100 us (92%)
  local copies, waits for them, and re-layouts  7.19 us (7%)
  between operations  1.34 us (1%)
    pallas_call x1, Pallas kernels, optimizer_step(): pl.pallas_call(step_kernel, name='optimizer_step', out_shape=(jax.ShapeDt...  88.3 us
    unnamed x18, local copies, waits for them, and re-layouts  7.19 us
    pallas_call x1, Pallas kernels, backward(): pl.pallas_call(backward_kernel, name='backward', out_shape=(jax.ShapeDtyp...  6.29 us
    pallas_call x1, Pallas kernels, forward(): pl.pallas_call(forward_kernel, name='forward', out_shape=(jax.ShapeDtypeS...  5.8 us

profile of v5, /device:TPU:1, one launch (start us, length us, event | category | flops | bytes accessed | tf_op | source)
XLA Modules:
  0.0 109.0 jit_solution(2492797084498138683)
XLA Ops:
  0.6 0.0 copy-start.7
  0.6 1.3 %copy.15.tiles = bf16[1,4,18,18,256]{4,3,2,1,0:T(8,128)(2,1)S(1)} copy(bf16[1,4,18,18,256]{4,1,3,2,0:T(4,128)(2,1)} %param.12) | data formatting | bytes 1327104 | tf_op args[2]
  2.6 0.0 copy-start
  2.6 0.9 copy-done
  3.5 0.0 copy-start.1
  3.5 0.9 copy-done.1
  4.5 0.0 copy-start.3
  4.5 0.9 copy-done.3
  5.4 0.0 copy-start.4
  5.4 0.7 copy-done.4
  6.1 0.0 copy-start.5
  6.1 0.7 copy-done.5
  6.7 0.0 copy-start.6
  6.8 0.7 copy-done.6
  7.4 6.3 %backward.1 = (bf16[8,4,28,16,128]{4,3,2,1,0:T(8,128)(2,1)S(1)}, f32[16,256]{1,0:T(8,128)S(1)}, f32[224,1]{1,0:T(8,128)S(1)}) custom-call(s32[224]{0:T(256)S(1)} %copy-done.4, s32[1]{0:T(128)S(6)} %copy.17.step_count, bf16[1,4,18,18,256]{4,3,2,1,0:T(8,128)(2,1)S(1)} %copy.15.tiles, bf16[512,256]{1,0:T(8,128)(2,1)S(1)} %copy-done, ...), custom_call_target="tpu_custom_call" | custom-call | tf_op jit(solution)/shard_map/backward/pallas_call | solution.py:588
  13.7 0.0 copy-start.2
  13.7 0.9 copy-done.2
  14.7 88.3 %optimizer_step.1 = (f32[7,32,256]{2,1,0:T(8,128)S(1)}, f32[7,32,256]{2,1,0:T(8,128)S(1)}, f32[7,32,1]{2,1,0:T(8,128)S(1)}, f32[8,256]{1,0:T(8,128)S(1)}, bf16[2,4,4,4,7,16,128]{6,5,4,3,2,1,0:T(8,128)(2,1)S(1)}) custom-call(bf16[2,4,4,4,7,16,128]{6,5,4,3,2,1,0:T(8,128)(2,1)S(1)} %bitcast.10, f32[16,256]{1,0:T(8,128)S(1)} %get-tuple-element.19.aux, ...), custom_call_target="tpu_custom_call" | custom-call | tf_op jit(solution)/shard_map/optimizer_step/pallas_call | solution.py:443
  103.0 0.0 copy-done.7
  103.0 0.1 copy.16.tiles
  103.2 5.8 %forward.1 = (bf16[512,256]{1,0:T(8,128)(2,1)}, f32[7,32,256]{2,1,0:T(8,128)}, f32[7,32,256]{2,1,0:T(8,128)}, f32[1,224]{1,0:T(1,128)}, f32[2,256]{1,0:T(2,128)}) custom-call(s32[224]{0:T(256)S(1)} %copy-done.4, bf16[1,4,18,18,256]{4,3,2,1,0:T(8,128)(2,1)S(1)} %copy.16.tiles, bf16[8,4,28,16,128]{4,3,2,1,0:T(8,128)(2,1)S(1)} %bitcast.9, ...), custom_call_target="tpu_custom_call" | custom-call | tf_op jit(solution)/shard_map/forward/pallas_call | solution.py:675
Async XLA Ops:
  0.6 102.4 %copy-start.7 = (bf16[1,4,18,18,256]{4,1,3,2,0:T(4,128)(2,1)S(1)}, bf16[1,4,18,18,256]{4,1,3,2,0:T(4,128)(2,1)}, u32[]{:S(2)}) copy-start(bf16[1,4,18,18,256]{4,1,3,2,0:T(4,128)(2,1)} %param.19) | copy-start | bytes 1990660
  2.6 1.0 copy-start
  3.5 0.9 copy-start.1
  4.5 0.9 copy-start.3
  5.4 0.7 copy-start.4
  6.1 0.7 copy-start.5
  6.7 0.7 copy-start.6
  13.7 0.9 copy-start.2

commit v6 on v5

--- a/solution.py
+++ b/solution.py
@@ -27,11 +27,13 @@
     aux,
     row_in,
     master,
+    next_tiles,
     update,
     new_master,
     new_row,
     new_col,
     weights,
+    next_shifted,
     core_in,
     first_sum,
     first_half,
@@ -131,7 +133,7 @@
     bf16 = jnp.bfloat16
 
     def add_into(dst, count, reads):
-        @pl.loop(0, count)
+        @pl.loop(0, count, unroll=count)
         def _(step):
             total = reads[0](step).astype(f32)
             for read in reads[1:]:
@@ -272,6 +274,7 @@
     ).astype(bf16)
 
     h_copies = [send(h_in.at[zh], h_in.at[zh], dev_h(d)) for d in (2, 1, 3)]
+    shift_columns(next_tiles, next_shifted)
     for copy in h_copies:
         copy.wait_recv()
     grad[x] = (
@@ -435,7 +438,7 @@
 VMEM_GRANT = 28 * 1024 * 1024
 
 
-def optimizer_step(term, aux, row_in, master):
+def optimizer_step(term, aux, row_in, master, next_tiles):
     f32 = jnp.float32
     bf16 = jnp.bfloat16
     tile = (OWN, 16, 128)
@@ -449,9 +452,10 @@
             jax.ShapeDtypeStruct((OWN, 32, 1), f32),
             jax.ShapeDtypeStruct((8, 256), f32),
             jax.ShapeDtypeStruct((2, 4, 4, 4) + tile, bf16),
+            jax.ShapeDtypeStruct((3, FR + 2, HW + 2, HW, CI), bf16),
         ),
-        in_specs=[vmem] * 4,
-        out_specs=[vmem] * 5,
+        in_specs=[vmem] * 5,
+        out_specs=[vmem] * 6,
         scratch_shapes=[
             pltpu.VMEM((4, 4, 4) + tile, bf16),
             pltpu.VMEM((2, 4, 4, 2) + tile, bf16),
@@ -474,7 +478,7 @@
         compiler_params=pltpu.CompilerParams(
             collective_id=0, has_side_effects=True, vmem_limit_bytes=VMEM_GRANT
         ),
-    )(term, aux, row_in, master)
+    )(term, aux, row_in, master, next_tiles)
 
 
 def shift_columns(tiles, shifted):
@@ -618,7 +622,7 @@
 
 def forward_kernel(
     order,
-    tiles,
+    shifted,
     gathered,
     update_in,
     master_in,
@@ -629,7 +633,6 @@
     master,
     new_row,
     new_col,
-    shifted,
     kernels,
     hidden,
 ):
@@ -641,7 +644,6 @@
     new_col[...] = col_in[0:2, :]
     update[...] = update_in[...]
     master[...] = master_in[...]
-    shift_columns(tiles, shifted)
 
     def place(block, outer, inner):
         for q in range(4):
@@ -667,7 +669,7 @@
         output[rows, :] = jnp.dot(acted, pointwise, preferred_element_type=f32).astype(jnp.bfloat16)
 
 
-def forward(block_order, next_tiles, gathered, update, master, row, col):
+def forward(block_order, shifted, gathered, update, master, row, col):
     bf16 = jnp.bfloat16
     f32 = jnp.float32
     vmem = pl.BlockSpec(memory_space=pltpu.VMEM)
@@ -685,12 +687,11 @@
         in_specs=[smem] + [vmem] * 6,
         out_specs=[vmem] * 5,
         scratch_shapes=[
-            pltpu.VMEM((3, FR + 2, HW + 2, HW, CI), bf16),
             pltpu.VMEM((NB, 2, 16, CO), bf16),
             pltpu.VMEM((FR * HW * HW, CO), f32),
         ],
         compiler_params=pltpu.CompilerParams(vmem_limit_bytes=VMEM_GRANT),
-    )(block_order, next_tiles, gathered, update, master, row, col)
+    )(block_order, shifted, gathered, update, master, row, col)
 
 
 def shards(
@@ -716,12 +717,16 @@
         row_moment,
     )
     term = term.reshape(2, 4, 4, 4, OWN, 16, 128)
-    update, new_master, new_row, new_col, gathered = optimizer_step(
-        term, aux, row_column.reshape(OWN, BLK, 1), master_rows.reshape(OWN, BLK, CO)
+    update, new_master, new_row, new_col, gathered, shifted = optimizer_step(
+        term,
+        aux,
+        row_column.reshape(OWN, BLK, 1),
+        master_rows.reshape(OWN, BLK, CO),
+        next_tiles,
     )
     next_output, update, new_master, new_row, new_col = forward(
         block_order,
-        next_tiles,
+        shifted,
         gathered.reshape(8, 4, 28, 16, 128),
         update,
         new_master,

time: 109 us -> 109 us (level)
    unnamed x18 -> x16, local copies, waits for them, and re-layouts: 7.19 us -> 7.28 us
where the time goes in v6:
time: 109 us; the launch traced here: 108 us
  Pallas kernels  99.7 us (91%)
  local copies, waits for them, and re-layouts  7.28 us (7%)
  between operations  1.37 us (1%)
    pallas_call x1, Pallas kernels, optimizer_step(): pl.pallas_call(step_kernel, name='optimizer_step', out_shape=(jax.ShapeDt...  88.3 us
    unnamed x16, local copies, waits for them, and re-layouts  7.28 us
    pallas_call x1, Pallas kernels, backward(): pl.pallas_call(backward_kernel, name='backward', out_shape=(jax.ShapeDtyp...  6.27 us
    pallas_call x1, Pallas kernels, forward(): pl.pallas_call(forward_kernel, name='forward', out_shape=(jax.ShapeDtypeS...  5.09 us

profile of v6, /device:TPU:1, one launch (start us, length us, event | category | flops | bytes accessed | tf_op | source)
XLA Modules:
  0.0 108.3 jit_solution(7108709928107541572)
XLA Ops:
  0.6 0.0 copy-start.2
  1.3 1.2 %copy.15.tiles = bf16[1,4,18,18,256]{4,3,2,1,0:T(8,128)(2,1)S(1)} copy(bf16[1,4,18,18,256]{4,1,3,2,0:T(4,128)(2,1)} %param.12) | data formatting | bytes 1327104 | tf_op args[2]
  2.6 1.2 %copy.16.next_tiles = bf16[1,4,18,18,256]{4,3,2,1,0:T(8,128)(2,1)S(1)} copy(bf16[1,4,18,18,256]{4,1,3,2,0:T(4,128)(2,1)} %param.19) | data formatting | bytes 1327104 | tf_op args[9]
  3.8 0.0 copy-start
  3.8 0.9 copy-done
  4.7 0.0 copy-start.1
  4.7 0.9 copy-done.1
  5.7 0.0 copy-start.3
  5.7 0.9 copy-done.3
  6.6 0.0 copy-start.4
  6.6 0.7 copy-done.4
  7.3 0.0 copy-start.5
  7.3 0.7 copy-done.5
  7.9 0.0 copy-start.6
  7.9 0.7 copy-done.6
  8.6 6.3 %backward.1 = (bf16[8,4,28,16,128]{4,3,2,1,0:T(8,128)(2,1)S(1)}, f32[16,256]{1,0:T(8,128)S(1)}, f32[224,1]{1,0:T(8,128)S(1)}) custom-call(s32[224]{0:T(256)S(1)} %copy-done.4, s32[1]{0:T(128)S(6)} %copy.17.step_count, bf16[1,4,18,18,256]{4,3,2,1,0:T(8,128)(2,1)S(1)} %copy.15.tiles, bf16[512,256]{1,0:T(8,128)(2,1)S(1)} %copy-done, ...), custom_call_target="tpu_custom_call" | custom-call | tf_op jit(solution)/shard_map/backward/pallas_call | solution.py:592
  14.9 0.0 copy-done.2
  14.9 88.3 %optimizer_step.1 = (f32[7,32,256]{2,1,0:T(8,128)S(1)}, f32[7,32,256]{2,1,0:T(8,128)S(1)}, f32[7,32,1]{2,1,0:T(8,128)S(1)}, f32[8,256]{1,0:T(8,128)S(1)}, bf16[2...) custom-call(bf16[2,4,4,4,7,16,128]{6,5,4,3,2,1,0:T(8,128)(2,1)S(1)} %bitcast.10, ...), custom_call_target="tpu_custom_call" | custom-call | tf_op jit(solution)/shard_map/optimizer_step/pallas_call | solution.py:446
  103.2 5.1 %forward.1 = (bf16[512,256]{1,0:T(8,128)(2,1)}, f32[7,32,256]{2,1,0:T(8,128)}, f32[7,32,256]{2,1,0:T(8,128)}, f32[1,224]{1,0:T(1,128)}, f32[2,256]{1,0:T(2,128)}) custom-call(s32[224]{0:T(256)S(1)} %copy-done.4, bf16[3,4,18,16,256]{4,3,2,1,0:T(8,128)(2,1)S(1)} %get-tuple-element.22.shifted, bf16[8,4,28,16,128]{4,3,2,1,0:T(8,128)(2,1)S(1)} %bitcast.9, ...), custom_call_target="tpu_custom_call" | custom-call | tf_op jit(solution)/shard_map/forward/pallas_call | solution.py:677
Async XLA Ops:
  0.6 14.3 %copy-start.2 = (f32[224,256]{1,0:T(8,128)S(1)}, f32[224,256]{1,0:T(8,128)}, u32[]{:S(2)}) copy-start(f32[224,256]{1,0:T(8,128)} %param.16) | copy-start | bytes 688132
  3.8 1.0 copy-start
  4.7 0.9 copy-start.1
  5.7 0.9 copy-start.3
  6.6 0.7 copy-start.4
  7.3 0.7 copy-start.5
  7.9 0.7 copy-start.6
